TPU v7x, 256 devices: a whole 4x4x8 slice. The times are simulated.
256 devices in a mesh: req: 32 (over y, z_hi, core), tp: 8 (over z_lo, x).
Axes of the slice: x: 4, y: 4, z: 8 (z_hi: 4, z_lo: 2; z = z_hi * 2 + z_lo), core: 2. Of those that a mesh axis runs over, the one named last changes fastest.
Arguments:
- tokens: bfloat16 [16384, 2048], P(('req', 'tp')), may hold values from -40 to 40, as said below
- attn_gain: float32 [2048], replicated, may hold values from 0.25 to 1.75
- w_query: bfloat16 [2048, 2048], P(None, 'tp'), may hold values from -0.125 to 0.125
- key_weight: bfloat16 [2048, 1024], P(None, 'tp'), may hold values from -0.125 to 0.125
- value_weight: bfloat16 [2048, 1024], P(None, 'tp'), may hold values from -0.125 to 0.125
- w_headgate: bfloat16 [2048, 16], P(None, 'tp'), may hold values from -0.125 to 0.125
- query_gain: float32 [128], replicated, may hold values from 1.3 to 2
- key_gain: float32 [128], replicated, may hold values from 1.3 to 2
- w_out: bfloat16 [2048, 2048], P('tp'), may hold values from -0.5 to 0.5
- mlp_gain: float32 [2048], replicated, may hold values from 0.25 to 1.75
- w_gate: bfloat16 [2048, 3072], P(None, 'tp'), may hold values from -0.125 to 0.125
- w_up: bfloat16 [2048, 3072], P(None, 'tp'), may hold values from -0.125 to 0.125
- w_down: bfloat16 [3072, 2048], P('tp'), may hold values from -0.109375 to 0.109375
- pooled_keys: bfloat16 [16384, 16, 8, 128], P(('req', 'tp')), may hold values from -150 to 150, as said below
- pooled_values: bfloat16 [16384, 16, 8, 128], P(('req', 'tp')), may hold values from -6 to 6
- sink_key_cache: bfloat16 [64, 4, 8, 128], P('req', None, 'tp'), may hold values from -12 to 12
- sink_value_cache: bfloat16 [64, 4, 8, 128], P('req', None, 'tp'), may hold values from -6 to 6
- cached_length: int32 [64], P('req'), may hold values from 0 to 32768, as said below
- valid_length: int32 [64], P('req'), may hold values from 1 to 256, as said below
- sink_position_count: int32 [64], P('req'), may hold values from 0 to 4, as said below
- window: int32 [64], P('req'), may hold values from 2048 to 4096, as said below
- page_slot: int32 [32, 512], P('req'), may hold values from 0 to 511, each once within a row
Outputs:
- out: float32 [16384, 2048], P(('req', 'tp'))
- app_keys: bfloat16 [16384, 8, 128], P('req', 'tp')
- app_values: bfloat16 [16384, 8, 128], P('req', 'tp')
Inputs may be any that keep to these rules, and one draw needn't show every extreme that they name: `tokens`: rows of the input; rows and features have unlike scales. `pooled_keys`: keys as the cache stores them. `cached_length`: short requests lie below 4096; some request has exactly 32768. `valid_length`: the rest of a span is padding; some request has exactly 256. `sink_position_count`: some request has exactly 4. `window`: some request has exactly 4096. `page_slot`: each row is a permutation.
All inputs are finite; a program needn't handle non-finite values.
Results may differ from a plain program's by a relative error of at most 0.02.
The roundings to bfloat16 on the way count: a program that leaves them out, or rounds other values in their place, can miss the bound.
Values may be sent and summed in bfloat16 or wider, within the bound.
A program may use at most 128 MiB of HBM per device.

v0:
```python
import math

import jax
import jax.numpy as jnp
from jax import lax
from jax.sharding import PartitionSpec as P

WINDOW_TOKENS = 4096
SPAN_TOKENS = 256


EPSILON = 1e-06
ROPE_BASE = 1000000.0
NEG_FILL = -1e30


def rms_rows(values, gain):
    mean_square = jnp.mean(values * values, axis=-1, keepdims=True)
    return values * lax.rsqrt(mean_square + EPSILON) * gain


def rotary(heads, positions):
    head_width = heads.shape[-1]
    half_width = head_width // 2
    freqs = ROPE_BASE ** (-2.0 * jnp.arange(half_width, dtype=jnp.float32) / head_width)
    angles = positions.astype(jnp.float32)[:, None] * freqs[None, :]
    cosine = jnp.cos(angles)[:, None, :]
    sine_part = jnp.sin(angles)[:, None, :]
    first_half = heads[..., :half_width]
    second_half = heads[..., half_width:]
    return jnp.concatenate(
        [
            first_half * cosine - second_half * sine_part,
            second_half * cosine + first_half * sine_part,
        ],
        axis=-1,
    )


def swiglu(normed_rows, w_gate, w_up):
    gate_part = jnp.dot(normed_rows, w_gate, preferred_element_type=jnp.float32)
    up_part = jnp.dot(normed_rows, w_up, preferred_element_type=jnp.float32)
    return (jax.nn.silu(gate_part) * up_part).astype(jnp.bfloat16)


def masked_max(scores, allowed):
    return jnp.max(jnp.where(allowed, scores, NEG_FILL), axis=-1)


def near_masks(cached, valid, sinks_used, reach, span_len, window_len, sink_len):
    offsets = jnp.arange(span_len, dtype=jnp.int32)
    sink_slots = jnp.arange(sink_len, dtype=jnp.int32)
    sink_ok = (sink_slots[None, :] < sinks_used[:, None]) & (
        sink_slots[None, :] < (cached - window_len)[:, None]
    )
    span_ok = (
        (offsets[None, None, :] < valid[:, None, None])
        & (offsets[None, None, :] <= offsets[None, :, None])
        & (
            (cached[:, None, None] + offsets[None, None, :] < sinks_used[:, None, None])
            | (offsets[None, :, None] - offsets[None, None, :] <= reach[:, None, None])
        )
    )
    return (sink_ok[:, None, None, None, :], span_ok[:, :, None, None, :])


def near_scores(query_vectors, sink_key_rows, fresh_keys, score_scale):
    sink_scores = (
        jnp.einsum(
            "rckgd,rskd->rckgs", query_vectors, sink_key_rows, preferred_element_type=jnp.float32
        )
        * score_scale
    )
    span_scores = (
        jnp.einsum(
            "rckgd,rtkd->rckgt", query_vectors, fresh_keys, preferred_element_type=jnp.float32
        )
        * score_scale
    )
    return (sink_scores, span_scores)


def attend_whole(
    query_vectors,
    sink_key_rows,
    sink_value_rows,
    window_key_rows,
    window_value_rows,
    fresh_keys,
    fresh_values,
    cached,
    valid,
    sinks_used,
    reach,
    score_scale,
):
    span_len = query_vectors.shape[1]
    window_len = window_key_rows.shape[1]
    sink_ok, span_ok = near_masks(
        cached, valid, sinks_used, reach, span_len, window_len, sink_key_rows.shape[1]
    )
    offsets = jnp.arange(span_len, dtype=jnp.int32)
    window_slots = jnp.arange(window_len, dtype=jnp.int32)
    key_positions = cached[:, None] - window_len + window_slots[None, :]
    window_ok = (key_positions[:, None, :] >= 0) & (
        (key_positions[:, None, :] < sinks_used[:, None, None])
        | (
            (window_len - window_slots)[None, None, :] + offsets[None, :, None]
            <= reach[:, None, None]
        )
    )
    window_ok = window_ok[:, :, None, None, :]
    sink_scores, span_scores = near_scores(query_vectors, sink_key_rows, fresh_keys, score_scale)
    window_scores = (
        jnp.einsum(
            "rckgd,rwkd->rckgw", query_vectors, window_key_rows, preferred_element_type=jnp.float32
        )
        * score_scale
    )
    highest = jnp.maximum(
        jnp.maximum(masked_max(sink_scores, sink_ok), masked_max(window_scores, window_ok)),
        masked_max(span_scores, span_ok),
    )[..., None]
    sink_weights = jnp.where(sink_ok, jnp.exp(sink_scores - highest), 0.0)
    window_weights = jnp.where(window_ok, jnp.exp(window_scores - highest), 0.0)
    span_weights = jnp.where(span_ok, jnp.exp(span_scores - highest), 0.0)
    total = (
        jnp.sum(sink_weights, axis=-1)
        + jnp.sum(window_weights, axis=-1)
        + jnp.sum(span_weights, axis=-1)
    )
    summed = jnp.einsum(
        "rckgs,rskd->rckgd",
        sink_weights.astype(jnp.bfloat16),
        sink_value_rows,
        preferred_element_type=jnp.float32,
    )
    summed = summed + jnp.einsum(
        "rckgw,rwkd->rckgd",
        window_weights.astype(jnp.bfloat16),
        window_value_rows,
        preferred_element_type=jnp.float32,
    )
    summed = summed + jnp.einsum(
        "rckgt,rtkd->rckgd",
        span_weights.astype(jnp.bfloat16),
        fresh_values,
        preferred_element_type=jnp.float32,
    )
    return summed / total[..., None]


def body(
    tokens,
    attn_gain,
    w_query,
    key_weight,
    value_weight,
    w_headgate,
    query_gain,
    key_gain,
    w_out,
    mlp_gain,
    w_gate,
    w_up,
    w_down,
    pooled_keys,
    pooled_values,
    sink_key_cache,
    sink_value_cache,
    cached_length,
    valid_length,
    sink_position_count,
    window,
    page_slot,
):
    head_dim = query_gain.shape[0]
    heads_dev = w_query.shape[1] // head_dim
    kv_dev = key_weight.shape[1] // head_dim
    group_size = heads_dev // kv_dev
    requests_dev = cached_length.shape[0]
    window_len = WINDOW_TOKENS
    span_len = SPAN_TOKENS
    rows_own = tokens.shape[0]
    score_scale = 1.0 / math.sqrt(head_dim)
    tp_index = lax.axis_index("tp")
    all_rows = lax.all_gather(tokens, "tp", axis=0, tiled=True)
    residual = all_rows.astype(jnp.float32)
    normalized_input = rms_rows(residual, attn_gain).astype(jnp.bfloat16)
    rows_total = normalized_input.shape[0]
    offsets = jnp.arange(span_len, dtype=jnp.int32)
    positions = (cached_length[:, None] + offsets[None, :]).reshape(rows_total)
    query_vectors = jnp.dot(normalized_input, w_query, preferred_element_type=jnp.float32).reshape(
        rows_total, heads_dev, head_dim
    )
    query_vectors = rotary(rms_rows(query_vectors, query_gain), positions).astype(jnp.bfloat16)
    fresh_keys = jnp.dot(normalized_input, key_weight, preferred_element_type=jnp.float32).reshape(
        rows_total, kv_dev, head_dim
    )
    fresh_keys = rotary(rms_rows(fresh_keys, key_gain), positions).astype(jnp.bfloat16)
    fresh_values = (
        jnp.dot(normalized_input, value_weight, preferred_element_type=jnp.float32)
        .astype(jnp.bfloat16)
        .reshape(rows_total, kv_dev, head_dim)
    )
    headgate = jax.nn.sigmoid(
        jnp.dot(normalized_input, w_headgate, preferred_element_type=jnp.float32)
    )
    present = (offsets[None, :] < valid_length[:, None]).reshape(rows_total)[:, None, None]
    app_keys = jnp.where(present, fresh_keys, jnp.zeros_like(fresh_keys))
    app_values = jnp.where(present, fresh_values, jnp.zeros_like(fresh_values))
    query_blocks = query_vectors.reshape(requests_dev, span_len, kv_dev, group_size, head_dim)
    key_blocks = fresh_keys.reshape(requests_dev, span_len, kv_dev, head_dim)
    value_blocks = fresh_values.reshape(requests_dev, span_len, kv_dev, head_dim)
    arrived_keys, arrived_values = (
        lax.all_to_all(pooled_keys, "tp", split_axis=2, concat_axis=0, tiled=True),
        lax.all_to_all(pooled_values, "tp", split_axis=2, concat_axis=0, tiled=True),
    )
    window_key_rows = jnp.take(arrived_keys, page_slot[0], axis=0).reshape(
        requests_dev, window_len, kv_dev, head_dim
    )
    window_value_rows = jnp.take(arrived_values, page_slot[0], axis=0).reshape(
        requests_dev, window_len, kv_dev, head_dim
    )
    mixture = attend_whole(
        query_blocks,
        sink_key_cache,
        sink_value_cache,
        window_key_rows,
        window_value_rows,
        key_blocks,
        value_blocks,
        cached_length,
        valid_length,
        sink_position_count,
        window,
        score_scale,
    )
    mixture = mixture.reshape(rows_total, heads_dev, head_dim)
    heads_out = (
        (mixture * headgate[..., None])
        .astype(jnp.bfloat16)
        .reshape(rows_total, heads_dev * head_dim)
    )
    attn = lax.psum(
        jnp.dot(heads_out, w_out, preferred_element_type=jnp.float32).astype(jnp.bfloat16), "tp"
    ).astype(jnp.float32)
    middle = residual + attn
    hidden = swiglu(rms_rows(middle, mlp_gain).astype(jnp.bfloat16), w_gate, w_up)
    branch = lax.psum(
        jnp.dot(hidden, w_down, preferred_element_type=jnp.float32).astype(jnp.bfloat16), "tp"
    ).astype(jnp.float32)
    row_start = tp_index * rows_own
    output = lax.dynamic_slice_in_dim(middle, row_start, rows_own, 0) + lax.dynamic_slice_in_dim(
        branch, row_start, rows_own, 0
    )
    return (output, app_keys, app_values)


def solution(mesh):
    in_specs = (
        P(("req", "tp"), None),
        P(),
        P(None, "tp"),
        P(None, "tp"),
        P(None, "tp"),
        P(None, "tp"),
        P(),
        P(),
        P("tp", None),
        P(),
        P(None, "tp"),
        P(None, "tp"),
        P("tp", None),
        P(("req", "tp"), None, None, None),
        P(("req", "tp"), None, None, None),
        P("req", None, "tp", None),
        P("req", None, "tp", None),
        P("req"),
        P("req"),
        P("req"),
        P("req"),
        P("req", None),
    )
    out_specs = (P(("req", "tp"), None), P("req", "tp", None), P("req", "tp", None))
    return jax.shard_map(body, mesh=mesh, in_specs=in_specs, out_specs=out_specs, check_vma=False)
```

profile of v0, /device:TPU:16, one launch (start us, length us, event | category | flops | bytes accessed | tf_op | source)
XLA Modules:
  0.0 336.9 jit_solution(11308946592861896893)
XLA Ops:
  7.2 0.7 all-gather.2.cloned.1.call-update
  7.9 3.2 copy.39
  11.1 5.8 %all-to-all-start.1 = ((bf16[64,16,8,128]{3,1,0,2:T(8,128)(2,1)}), bf16[64,16,8,128]{3,1,0,2:T(8,128)(2,1)}, u32[]{:S(2)}, u32[]{:S(2)}) async-start(bf16[64,16,8,128]{3,1,0,2:T(8,128)(2,1)} %copy.39), calls=%async_computation.1 | async-start | bytes 4194304 | tf_op jit(solution)/shard_map/all_to_all | solution.py:217
  17.2 3.2 copy.36
  21.3 0.6 iota_add_fusion
  22.0 4.6 %or_and_fusion = pred[2,256,4096]{1,2,0:T(8,128)(4,1)} fusion(s32[256,4096]{0,1:T(8,128)S(1)} %iota_add_fusion, s32[2]{0:T(128)S(1)} %copy-done.16, pred[2,4096]{1,0:T(4,128)(4,1)S(1)} %get-tuple-element.21, pred[2,4096]{1,0:T(4,128)(4,1)S(1)} %get-tuple-element.20), kind=kLoop, calls=%fused_computation.12 | loop fusion | flops 6291456 | bytes 6307848 | tf_op jit(solution)/shard_map/and | solution.py:105
  26.5 22.6 %all-to-all-done.1 = bf16[64,16,8,128]{3,1,0,2:T(8,128)(2,1)} async-done(((bf16[64,16,8,128]{3,1,0,2:T(8,128)(2,1)}), bf16[64,16,8,128]{3,1,0,2:T(8,128)(2,1)}, u32[]{:S(2)}, u32[]{:S(2)}) %all-to-all-start.1) | async-done | bytes 2097184 | tf_op jit(solution)/shard_map/all_to_all | solution.py:217
  49.2 5.8 %all-to-all-start = ((bf16[64,16,8,128]{3,1,0,2:T(8,128)(2,1)}), bf16[64,16,8,128]{3,1,0,2:T(8,128)(2,1)}, u32[]{:S(2)}, u32[]{:S(2)}) async-start(bf16[64,16,8,128]{3,1,0,2:T(8,128)(2,1)} %copy.36), calls=%async_computation | async-start | bytes 4194304 | tf_op jit(solution)/shard_map/all_to_all | solution.py:216
  55.1 30.3 %all-gather.2.cloned.1.call-done = bf16[512,2048]{1,0:T(8,128)(2,1)} async-done(((bf16[64,2048]{1,0:T(8,128)(2,1)}), bf16[512,2048]{1,0:T(8,128)(2,1)}) %all-gather.2.cloned.1.call-update) | async-done | bytes 2097168 | tf_op jit(solution)/shard_map/all_gather | solution.py:187
  85.3 2.2 fusion.9
  88.2 1.4 copy-done.1
  89.5 0.7 fusion.20
  90.4 2.6 multiply_reduce_fusion.1
  94.0 2.4 multiply_reduce_fusion.2
  97.4 4.0 %gather_fusion.1 = bf16[512,16,128]{2,1,0:T(8,128)(2,1)} fusion(bf16[512,16,128]{2,1,0:T(8,128)(2,1)} %bitcast.34, s32[1024]{0:T(1024)S(1)} %pad_clamp_fusion), kind=kCustom, calls=%fused_computation.1.clone | custom fusion | bytes 4196352 | tf_op jit(solution)/shard_map/jit(_take)/gather | solution.py:222
  101.5 2.3 convolution_convert_fusion.2
  103.8 4.0 %gather_fusion = bf16[512,16,128]{2,1,0:T(8,128)(2,1)} fusion(bf16[512,16,128]{2,1,0:T(8,128)(2,1)} %bitcast.11, s32[1024]{0:T(1024)S(1)} %pad_clamp_fusion), kind=kCustom, calls=%fused_computation.clone | custom fusion | bytes 4196352 | tf_op jit(solution)/shard_map/jit(_take)/gather | solution.py:219
  107.8 4.9 %bitcast_select_fusion.1 = (bf16[512,16,1,128]{3,1,0,2:T(8,128)(2,1)}, bf16[512,16,1,128]{3,1,0,2:T(8,128)(2,1)}) fusion(bf16[512,16,128]{2,1,0:T(8,128)(2,1)} %gather_fusion.1, pred[512]{0:T(512)(128)(4,1)S(1)} %compare_and_fusion, bf16[512,16,128]{2,1,0:T(8,128)(2,1)} %gather_fusion), kind=kLoop, calls=%fused_computation.24 | loop fusion | flops 2097152 | bytes 8389120 | tf_op jit(solution)/shard_map/jit(_take)/select_n | solution.py:222
  112.9 4.1 %fusion = (f32[2,256,2]{1,2,0:T(2,128)S(1)}, f32[2,4096,256,2]{2,1,3,0:T(8,128)S(1)}) fusion(pred[2,256,4096]{1,2,0:T(8,128)(4,1)S(1)} %copy-done.5, bf16[2,4096,128,1]{2,1,3,0:T(8,128)(2,1)} %bitcast.160, bf16[2,256,2,64]{3,1,2,0:T(8,128)(2,1)S(1)} %copy.35, bf16[2,256,2,64]{3,1,2,0:T(8,128)(2,1)S(1)} %copy.34), kind=kOutput, calls=%fused_computation.4 | convolution fusion | flops 1086848000 | bytes 21237760 | tf_op jit(solution)/shard_map/rckgd,rwkd->rckgw/dot_general | solution.py:115
  118.1 3.9 %fusion.3 = f32[2,256,2]{1,2,0:T(2,128)S(1)} fusion(f32[2,4096,256,2]{2,1,3,0:T(8,128)S(1)} %get-tuple-element.31, f32[2,256,2]{1,2,0:T(2,128)S(1)} %maximum_maximum_fusion, pred[2,256,4096]{1,2,0:T(8,128)(4,1)S(1)} %copy-done.5), kind=kLoop, calls=%fused_computation.7 | loop fusion | flops 16776192 | bytes 18882560 | tf_op jit(solution)/shard_map/reduce_sum | solution.py:129
  122.1 0.7 copy-done.4
  122.8 9.7 %fusion.6 = f32[2,128,256,2]{1,2,3,0:T(8,128)S(1)} fusion(bf16[2,4096,128,1]{2,1,3,0:T(8,128)(2,1)} %bitcast.159, f32[2,4096,256,2]{2,1,3,0:T(8,128)} %copy-done.4, f32[2,256,2]{1,2,0:T(2,128)S(1)} %maximum_maximum_fusion, pred[2,256,4096]{1,2,0:T(8,128)(4,1)} %or_and_fusion), kind=kOutput, calls=%fused_computation.10 | convolution fusion | flops 1090519040 | bytes 21499904 | tf_op jit(solution)/shard_map/rckgw,rwkd->rckgd/dot_general | solution.py:138
  133.4 0.6 mul.265
  134.0 2.0 convolution_convert_fusion
  136.4 90.2 %all-reduce.3.cloned.1.call-done = bf16[512,2048]{1,0:T(8,128)(2,1)} async-done(((bf16[512,2048]{1,0:T(8,128)(2,1)}), bf16[512,2048]{1,0:T(8,128)(2,1)}) %all-reduce.3.cloned.1.call-update) | async-done | bytes 2097168 | tf_op jit(solution)/shard_map/psum | solution.py:245
  226.5 5.0 %multiply_reduce_fusion = (f32[512]{0:T(512)S(1)}, f32[512,2048]{1,0:T(8,128)}) fusion(bf16[512,2048]{1,0:T(8,128)(2,1)} %all-reduce.3.cloned.1.call-done, bf16[512,2048]{1,0:T(8,128)(2,1)} %all-gather.2.cloned.1.call-done), kind=kLoop, calls=%fused_computation.20 | loop fusion | flops 5242368 | bytes 8390656 | tf_op jit(solution)/shard_map/reduce_sum | solution.py:18
  231.5 2.7 fusion.66
  234.3 6.4 %convolution_convert_fusion.1 = bf16[512,2048]{1,0:T(8,128)(2,1)} fusion(bf16[384,2048]{1,0:T(8,128)(2,1)S(1)} %copy-done, bf16[2048,384]{1,0:T(8,128)(2,1)} %param.35, f32[512,384]{1,0:T(8,128)S(1)} %fusion.66, f32[2048]{0:T(1024)S(1)} %copy-done.20, f32[512]{0:T(512)S(1)} %add_rsqrt_fusion.1, bf16[512,2048]{1,0:T(8,128)(2,1)} %all-gather.2.cloned.1.call-done, ...), kind=kOutput, calls=%fused_computation.23 | convolution fusion | flops 1619132416 | bytes 10233856 | tf_op jit(solution)/shard_map/dot_general | solution.py:251
  240.8 0.8 copy.48
  241.5 0.8 select_bitcast_fusion
  242.3 86.1 %all-reduce.5.cloned.1.call-done = bf16[512,2048]{1,0:T(8,128)(2,1)} async-done(((bf16[512,2048]{1,0:T(8,128)(2,1)}), bf16[512,2048]{1,0:T(8,128)(2,1)}) %all-reduce.5.cloned.1.call-update) | async-done | bytes 2097168 | tf_op jit(solution)/shard_map/psum | solution.py:250
  328.5 1.9 convert_add_fusion.1
  (90 shorter events, 6.5 us)
Async XLA Ops:
  7.2 227.1 %copy-start = (bf16[384,2048]{1,0:T(8,128)(2,1)S(1)}, bf16[384,2048]{1,0:T(8,128)(2,1)}, u32[]{:S(2)}) copy-start(bf16[384,2048]{1,0:T(8,128)(2,1)} %param.36) | copy-start | bytes 4718596
  7.2 78.2 %all-gather.2.cloned.1.call-start = ((), (), s32[]{:S(2)}) async-start(), calls=%async_computation.2 | async-start | bytes 2359296 | tf_op jit(solution)/shard_map/all_gather | solution.py:187
  11.1 5.8 %copy-start.15 = (s32[2]{0:T(128)S(1)}, s32[2]{0:T(128)}, u32[]{:S(2)}) copy-start(s32[2]{0:T(128)} %param.41) | copy-start | bytes 28
  11.1 5.9 %copy-start.12 = (s32[1,512]{1,0:T(1,128)S(1)}, s32[1,512]{1,0:T(1,128)}, u32[]{:S(2)}) copy-start(s32[1,512]{1,0:T(1,128)} %param.45) | copy-start | bytes 6148
  11.1 5.9 %copy-start.14 = (s32[2]{0:T(128)S(1)}, s32[2]{0:T(128)}, u32[]{:S(2)}) copy-start(s32[2]{0:T(128)} %param.43) | copy-start | bytes 28
  11.1 6.0 %copy-start.19 = (s32[2]{0:T(128)S(1)}, s32[2]{0:T(128)}, u32[]{:S(2)}) copy-start(s32[2]{0:T(128)} %param.42) | copy-start | bytes 28
  11.1 38.1 %all-to-all-start.1 = ((bf16[64,16,8,128]{3,1,0,2:T(8,128)(2,1)}), bf16[64,16,8,128]{3,1,0,2:T(8,128)(2,1)}, u32[]{:S(2)}, u32[]{:S(2)}) async-start(bf16[64,16,8,128]{3,1,0,2:T(8,128)(2,1)} %copy.39), calls=%async_computation.1 | async-start | bytes 4194304 | tf_op jit(solution)/shard_map/all_to_all | solution.py:217
  17.2 3.8 %copy-start.16 = (s32[2]{0:T(128)S(1)}, s32[2]{0:T(128)}, u32[]{:S(2)}) copy-start(s32[2]{0:T(128)} %param.44) | copy-start | bytes 28
  49.2 54.6 %all-to-all-start = ((bf16[64,16,8,128]{3,1,0,2:T(8,128)(2,1)}), bf16[64,16,8,128]{3,1,0,2:T(8,128)(2,1)}, u32[]{:S(2)}, u32[]{:S(2)}) async-start(bf16[64,16,8,128]{3,1,0,2:T(8,128)(2,1)} %copy.36), calls=%async_computation | async-start | bytes 4194304 | tf_op jit(solution)/shard_map/all_to_all | solution.py:216
  55.0 32.6 %copy-start.10 = (f32[2048]{0:T(1024)S(1)}, f32[2048]{0:T(1024)}, u32[]{:S(2)}) copy-start(f32[2048]{0:T(1024)} %param.25) | copy-start | bytes 24580
  55.0 171.5 %all-reduce.3.cloned.1.call-start = ((), (), s32[]{:S(2)}) async-start(), calls=%async_computation.3 | async-start | bytes 4194304 | tf_op jit(solution)/shard_map/psum | solution.py:245
  85.3 2.2 copy-start.2
  87.6 1.9 copy-start.11
  88.2 1.4 copy-start.1
  90.2 2.8 copy-start.17
  93.0 1.0 copy-start.8
  93.3 3.2 copy-start.18
  97.4 4.1 %copy-start.9 = (bf16[2048,128]{1,0:T(8,128)(2,1)S(1)}, bf16[2048,128]{1,0:T(8,128)(2,1)}, u32[]{:S(2)}) copy-start(bf16[2048,128]{1,0:T(8,128)(2,1)} %param.28) | copy-start | bytes 1572868
  107.8 4.9 %copy-start.13 = (bf16[2,4,1,128]{3,1,2,0:T(4,128)(2,1)S(1)}, bf16[2,4,1,128]{3,1,2,0:T(4,128)(2,1)}, u32[]{:S(2)}) copy-start(bf16[2,4,1,128]{3,1,2,0:T(4,128)(2,1)} %param.39) | copy-start | bytes 6148
  107.8 5.2 %copy-start.5 = (pred[2,256,4096]{1,2,0:T(8,128)(4,1)S(1)}, pred[2,256,4096]{1,2,0:T(8,128)(4,1)}, u32[]{:S(2)}) copy-start(pred[2,256,4096]{1,2,0:T(8,128)(4,1)} %or_and_fusion) | copy-start | bytes 6291460
  117.0 5.7 %copy-start.4 = (f32[2,4096,256,2]{2,1,3,0:T(8,128)}, f32[2,4096,256,2]{2,1,3,0:T(8,128)S(1)}, u32[]{:S(2)}) copy-start(f32[2,4096,256,2]{2,1,3,0:T(8,128)S(1)} %get-tuple-element.31) | copy-start | bytes 50331652
  122.8 9.8 %copy-start.21 = (bf16[2,4,1,128]{3,1,2,0:T(4,128)(2,1)S(1)}, bf16[2,4,1,128]{3,1,2,0:T(4,128)(2,1)}, u32[]{:S(2)}) copy-start(bf16[2,4,1,128]{3,1,2,0:T(4,128)(2,1)} %param.40) | copy-start | bytes 6148
  132.5 1.5 copy-start.7
  136.1 95.4 %copy-start.20 = (f32[2048]{0:T(1024)S(1)}, f32[2048]{0:T(1024)}, u32[]{:S(2)}) copy-start(f32[2048]{0:T(1024)} %param.33) | copy-start | bytes 24580
  136.1 192.4 %all-reduce.5.cloned.1.call-start = ((), (), s32[]{:S(2)}) async-start(), calls=%async_computation.4 | async-start | bytes 4194304 | tf_op jit(solution)/shard_map/psum | solution.py:250
  226.5 5.0 %copy-start.3 = (bf16[512,2048]{1,0:T(8,128)(2,1)S(1)}, bf16[512,2048]{1,0:T(8,128)(2,1)}, u32[]{:S(2)}) copy-start(bf16[512,2048]{1,0:T(8,128)(2,1)} %all-gather.2.cloned.1.call-done) | copy-start | bytes 6291460
  226.5 5.0 %copy-start.6 = (bf16[512,2048]{1,0:T(8,128)(2,1)S(1)}, bf16[512,2048]{1,0:T(8,128)(2,1)}, u32[]{:S(2)}) copy-start(bf16[512,2048]{1,0:T(8,128)(2,1)} %all-reduce.3.cloned.1.call-done) | copy-start | bytes 6291460
Sparse Core Ops, SparseCore 0:
  9.8 75.5 all-gather.1
  136.2 90.2 all-reduce.2
  240.8 87.5 all-reduce.4
where the time goes:
time: 338 us; the launch traced here: 337 us
  waiting for transfers between devices  230 us (68%)
  matrix products  34.5 us (10%)
  other arithmetic  26.8 us (8%)
  local copies, waits for them, and re-layouts  19.5 us (6%)
  between operations  14.2 us (4%)
  starting transfers between devices  12 us (4%)
    psum x1, waiting for transfers between devices, body(): lax.psum(jnp.dot(heads_out, w_out, preferred_element_type=jnp.float32).as...  90.2 us
    psum x1, waiting for transfers between devices, body(): lax.psum(jnp.dot(hidden, w_down, preferred_element_type=jnp.float32).asty...  86.1 us
    all_gather x1, waiting for transfers between devices, body(): all_rows = lax.all_gather(tokens, 'tp', axis=0, tiled=True)  30.3 us
    all_to_all x1, waiting for transfers between devices, body(): lax.all_to_all(pooled_values, 'tp', split_axis=2, concat_axis=0, tiled=True)  22.6 us
    dot_general x1, matrix products, attend_whole(): jnp.einsum('rckgw,rwkd->rckgd', window_weights.astype(jnp.bfloat16), wind...  9.68 us
    unnamed x48, local copies, waits for them, and re-layouts  9.64 us
    reduce_sum x2, other arithmetic, rms_rows(): mean_square = jnp.mean(values * values, axis=-1, keepdims=True)  7.22 us
  transfers between devices with their start and end apart: 5, of which 4 were waited for; matrix products, arithmetic and copies ran while one was open for 9% of the time, Pallas kernels for 0%

commit v1 on v0

--- a/solution.py
+++ b/solution.py
@@ -3,6 +3,8 @@
 import jax
 import jax.numpy as jnp
 from jax import lax
+from jax.experimental import pallas as pl
+from jax.experimental.pallas import tpu as pltpu
 from jax.sharding import PartitionSpec as P
 
 WINDOW_TOKENS = 4096
@@ -35,12 +37,6 @@
         ],
         axis=-1,
     )
-
-
-def swiglu(normed_rows, w_gate, w_up):
-    gate_part = jnp.dot(normed_rows, w_gate, preferred_element_type=jnp.float32)
-    up_part = jnp.dot(normed_rows, w_up, preferred_element_type=jnp.float32)
-    return (jax.nn.silu(gate_part) * up_part).astype(jnp.bfloat16)
 
 
 def masked_max(scores, allowed):
@@ -148,6 +144,373 @@
         preferred_element_type=jnp.float32,
     )
     return summed / total[..., None]
+
+
+MESH = pl.DeviceIdType.MESH
+ROWS = 64
+WIDTH = 2048
+
+
+def ring_place(shift, flip):
+    t = lax.axis_index("tp")
+    x = lax.rem(t, 4)
+    z = t // 4
+    plane = 1 - z if flip else z
+    return lax.rem(x + shift, 4) + 4 * plane
+
+
+def row_window(owner, first, count):
+    return pl.ds(pl.multiple_of(owner * ROWS + first, 16), count)
+
+
+class Mailer:
+    def __init__(self, send_sems, recv_sems):
+        self.send_sems, self.recv_sems = send_sems, recv_sems
+        self.slots = {}
+        self.sent = []
+
+    def slot(self, name):
+        return self.slots.setdefault(name, len(self.slots))
+
+    def send(self, name, src, dst, target):
+        k = self.slot(name)
+        copy = pltpu.make_async_remote_copy(
+            src_ref=src,
+            dst_ref=dst,
+            send_sem=self.send_sems.at[k],
+            recv_sem=self.recv_sems.at[k],
+            device_id={"tp": target},
+            device_id_type=MESH,
+        )
+        copy.start()
+        self.sent.append(copy)
+
+    def wait(self, name, dst):
+        k = self.slot(name)
+        pltpu.make_async_remote_copy(
+            src_ref=dst,
+            dst_ref=dst,
+            send_sem=self.send_sems.at[k],
+            recv_sem=self.recv_sems.at[k],
+            device_id={"tp": ring_place(0, True)},
+            device_id_type=MESH,
+        ).wait_recv()
+
+    def drain(self):
+        for copy in self.sent:
+            copy.wait_send()
+        self.sent = []
+
+
+def meet_neighbours():
+    barrier = pltpu.get_barrier_semaphore()
+    for shift, flip in ((1, False), (3, False), (0, True)):
+        pl.semaphore_signal(
+            barrier, inc=1, device_id={"tp": ring_place(shift, flip)}, device_id_type=MESH
+        )
+    pl.semaphore_wait(barrier, 3)
+
+
+def add_into(part, owner, first, count, arrived):
+    rows = row_window(owner, first, count)
+    part[rows, :] = (
+        part[rows, :].astype(jnp.float32) + arrived[...].astype(jnp.float32)
+    ).astype(jnp.bfloat16)
+
+
+class Scatter:
+    def __init__(self, mail, tag, part, h1, h2, zb, b1, b2, za):
+        self.mail, self.tag, self.part = mail, tag, part
+        self.h1, self.h2, self.zb, self.b1, self.b2, self.za = h1, h2, zb, b1, b2, za
+        self.right, self.left, self.across = ring_place(1, False), ring_place(3, False), ring_place(0, True)
+
+    def rows(self, shift, flip, first, count):
+        return self.part.at[row_window(ring_place(shift, flip), first, count), :]
+
+    def put(self, name, src, dst, target):
+        self.mail.send(self.tag + name, src, dst, target)
+
+    def got(self, name, dst):
+        self.mail.wait(self.tag + name, dst)
+
+    def start_x(self, flip):
+        f = int(flip)
+        self.put(f"h1r{f}", self.rows(2, flip, 0, 16), self.h1.at[0, f], self.right)
+        self.put(f"h1l{f}", self.rows(2, flip, 16, 16), self.h1.at[1, f], self.left)
+        self.put(f"h2r{f}1", self.rows(1, flip, 16, 16), self.h2.at[0, f, 1], self.right)
+        self.put(f"h2l{f}0", self.rows(3, flip, 0, 16), self.h2.at[1, f, 0], self.left)
+
+    def start_z(self):
+        for k, shift in enumerate((2, 1, 3, 0)):
+            self.put(f"zb{k}", self.rows(shift, True, 32, 32), self.zb.at[k], self.across)
+
+    def relay_x(self, flip):
+        f = int(flip)
+        self.got(f"h1r{f}", self.h1.at[0, f])
+        add_into(self.part, ring_place(1, flip), 0, 16, self.h1.at[0, f])
+        self.put(f"h2r{f}0", self.rows(1, flip, 0, 16), self.h2.at[0, f, 0], self.right)
+        self.got(f"h1l{f}", self.h1.at[1, f])
+        add_into(self.part, ring_place(3, flip), 16, 16, self.h1.at[1, f])
+        self.put(f"h2l{f}1", self.rows(3, flip, 16, 16), self.h2.at[1, f, 1], self.left)
+
+    def relay_z(self):
+        self.got("zb0", self.zb.at[0])
+        add_into(self.part, ring_place(2, False), 32, 32, self.zb.at[0])
+        self.put("b1r", self.rows(2, False, 32, 16), self.b1.at[0], self.right)
+        self.put("b1l", self.rows(2, False, 48, 16), self.b1.at[1], self.left)
+        self.got("zb1", self.zb.at[1])
+        add_into(self.part, ring_place(1, False), 32, 32, self.zb.at[1])
+        self.put("b2r1", self.rows(1, False, 48, 16), self.b2.at[0, 1], self.right)
+        self.got("zb2", self.zb.at[2])
+        add_into(self.part, ring_place(3, False), 32, 32, self.zb.at[2])
+        self.put("b2l0", self.rows(3, False, 32, 16), self.b2.at[1, 0], self.left)
+
+    def finish_relays(self):
+        for side, letter in ((0, "r"), (1, "l")):
+            for half in (0, 1):
+                self.got(f"h2{letter}1{half}", self.h2.at[side, 1, half])
+        rows = row_window(self.across, 0, 32)
+        self.part[rows, :] = (
+            self.part[rows, :].astype(jnp.float32)
+            + self.h2[0, 1].reshape(32, WIDTH).astype(jnp.float32)
+            + self.h2[1, 1].reshape(32, WIDTH).astype(jnp.float32)
+        ).astype(jnp.bfloat16)
+        self.put("za", self.rows(0, True, 0, 32), self.za, self.across)
+        self.got("b1r", self.b1.at[0])
+        add_into(self.part, ring_place(1, False), 32, 16, self.b1.at[0])
+        self.put("b2r0", self.rows(1, False, 32, 16), self.b2.at[0, 0], self.right)
+        self.got("b1l", self.b1.at[1])
+        add_into(self.part, ring_place(3, False), 48, 16, self.b1.at[1])
+        self.put("b2l1", self.rows(3, False, 48, 16), self.b2.at[1, 1], self.left)
+
+    def total(self):
+        me = ring_place(0, False)
+        f32 = jnp.float32
+        for side, letter in ((0, "r"), (1, "l")):
+            for half in (0, 1):
+                self.got(f"h2{letter}0{half}", self.h2.at[side, 0, half])
+        upper = (
+            self.part[row_window(me, 0, 32), :].astype(f32)
+            + self.h2[0, 0].reshape(32, WIDTH).astype(f32)
+            + self.h2[1, 0].reshape(32, WIDTH).astype(f32)
+        )
+        self.got("zb3", self.zb.at[3])
+        lower = self.part[row_window(me, 32, 32), :].astype(f32) + self.zb[3].astype(f32)
+        for side, letter in ((0, "r"), (1, "l")):
+            for half in (0, 1):
+                self.got(f"b2{letter}{half}", self.b2.at[side, half])
+        lower = (
+            lower
+            + self.b2[0].reshape(32, WIDTH).astype(f32)
+            + self.b2[1].reshape(32, WIDTH).astype(f32)
+        )
+        self.got("za", self.za)
+        upper = upper + self.za[...].astype(f32)
+        return upper, lower
+
+
+SCATTER_BUFFERS = [
+    ((2, 2, 16, WIDTH)),
+    ((2, 2, 2, 16, WIDTH)),
+    ((4, 32, WIDTH)),
+    ((2, 16, WIDTH)),
+    ((2, 2, 16, WIDTH)),
+    ((32, WIDTH)),
+]
+SCATTER_COPIES = 24
+
+
+class Gather:
+    def __init__(self, mail, tag, rows):
+        self.mail, self.tag, self.rows = mail, tag, rows
+        self.right, self.left, self.across = ring_place(1, False), ring_place(3, False), ring_place(0, True)
+
+    def part(self, shift, flip, first, count):
+        return self.rows.at[row_window(ring_place(shift, flip), first, count), :]
+
+    def put(self, name, place, target):
+        ref = self.part(*place)
+        self.mail.send(self.tag + name, ref, ref, target)
+
+    def got(self, name, place):
+        self.mail.wait(self.tag + name, self.part(*place))
+
+    def start(self):
+        self.put("z0", (0, False, 0, 32), self.across)
+        self.put("r0", (0, False, 32, 32), self.right)
+        self.put("l0", (0, False, 32, 32), self.left)
+        self.put("r1", (0, False, 0, 32), self.right)
+        self.put("l1", (0, False, 0, 32), self.left)
+        self.put("z1", (0, False, 32, 32), self.across)
+
+    def relay_near(self):
+        self.got("r0", (3, False, 32, 32))
+        self.put("r2", (3, False, 32, 16), self.right)
+        self.put("z2", (3, False, 32, 32), self.across)
+        self.got("l0", (1, False, 32, 32))
+        self.put("l2", (1, False, 48, 16), self.left)
+        self.put("z3", (1, False, 32, 32), self.across)
+        self.got("r1", (3, False, 0, 32))
+        self.put("r4", (3, False, 0, 16), self.right)
+        self.got("l1", (1, False, 0, 32))
+        self.put("l4", (1, False, 16, 16), self.left)
+        self.got("z0", (0, True, 0, 32))
+        self.put("r3", (0, True, 0, 32), self.right)
+        self.put("l3", (0, True, 0, 32), self.left)
+        self.got("r2", (2, False, 32, 16))
+        self.put("z4", (2, False, 32, 16), self.across)
+        self.got("l2", (2, False, 48, 16))
+        self.put("z5", (2, False, 48, 16), self.across)
+        self.got("r4", (2, False, 0, 16))
+        self.got("l4", (2, False, 16, 16))
+
+    def relay_far(self):
+        self.got("r3", (3, True, 0, 32))
+        self.put("r5", (3, True, 0, 16), self.right)
+        self.got("l3", (1, True, 0, 32))
+        self.put("l5", (1, True, 16, 16), self.left)
+
+    def finish(self):
+        self.got("r5", (2, True, 0, 16))
+        self.got("l5", (2, True, 16, 16))
+        self.got("z1", (0, True, 32, 32))
+        self.got("z2", (3, True, 32, 32))
+        self.got("z3", (1, True, 32, 32))
+        self.got("z4", (2, True, 32, 16))
+        self.got("z5", (2, True, 48, 16))
+
+
+GATHER_COPIES = 18
+
+
+def tail_kernel(
+    heads_ref,
+    tokens_ref,
+    gain_ref,
+    w_out_ref,
+    w_gate_ref,
+    w_up_ref,
+    w_down_ref,
+    out_ref,
+    w_out_vmem,
+    w_both_vmem,
+    w_down_vmem,
+    part_one,
+    part_two,
+    rows_mid,
+    middle,
+    *rest,
+):
+    buffers_one, buffers_two = rest[:6], rest[6:12]
+    load_sems, send_sems, recv_sems = rest[12:]
+    units = w_down_ref.shape[0]
+    loads = [
+        pltpu.make_async_copy(w_out_ref, w_out_vmem, load_sems.at[0]),
+        pltpu.make_async_copy(w_gate_ref, w_both_vmem.at[:, :units], load_sems.at[1]),
+        pltpu.make_async_copy(w_up_ref, w_both_vmem.at[:, units:], load_sems.at[2]),
+        pltpu.make_async_copy(w_down_ref, w_down_vmem, load_sems.at[3]),
+    ]
+    for load in loads:
+        load.start()
+    meet_neighbours()
+    mail = Mailer(send_sems, recv_sems)
+    plane = lax.axis_index("tp") // 4
+    half_rows = 4 * ROWS
+
+    def half(flip):
+        return pl.ds(pl.multiple_of((1 - plane if flip else plane) * half_rows, half_rows), half_rows)
+
+    scatter = Scatter(mail, "a", part_one, *buffers_one)
+    loads[0].wait()
+
+    def project(flip):
+        rows = half(flip)
+        part_one[rows, :] = jnp.dot(
+            heads_ref[rows, :], w_out_vmem[...], preferred_element_type=jnp.float32
+        ).astype(jnp.bfloat16)
+
+    project(True)
+    scatter.start_z()
+    scatter.start_x(True)
+    project(False)
+    scatter.start_x(False)
+    scatter.relay_x(True)
+    scatter.relay_x(False)
+    scatter.relay_z()
+    scatter.finish_relays()
+    upper, lower = scatter.total()
+    me = ring_place(0, False)
+    for first, attn in ((0, upper), (32, lower)):
+        mid = tokens_ref[first : first + 32, :].astype(jnp.float32) + attn
+        middle[first : first + 32, :] = mid
+        mean_square = jnp.mean(mid * mid, axis=-1, keepdims=True)
+        rows_mid[row_window(me, first, 32), :] = (
+            mid * lax.rsqrt(mean_square + EPSILON) * gain_ref[...]
+        ).astype(jnp.bfloat16)
+    gather = Gather(mail, "g", rows_mid)
+    gather.start()
+    gather.relay_near()
+    for load in loads[1:]:
+        load.wait()
+
+    def feed(flip):
+        rows = half(flip)
+        both = jnp.dot(rows_mid[rows, :], w_both_vmem[...], preferred_element_type=jnp.float32)
+        gate, up = both[:, :units], both[:, units:]
+        hidden = (gate / (1.0 + jnp.exp(-gate)) * up).astype(jnp.bfloat16)
+        part_two[rows, :] = jnp.dot(
+            hidden, w_down_vmem[...], preferred_element_type=jnp.float32
+        ).astype(jnp.bfloat16)
+
+    scatter = Scatter(mail, "b", part_two, *buffers_two)
+    gather.relay_far()
+    feed(False)
+    scatter.start_x(False)
+    gather.finish()
+    feed(True)
+    scatter.start_z()
+    scatter.start_x(True)
+    scatter.relay_x(False)
+    scatter.relay_x(True)
+    scatter.relay_z()
+    scatter.finish_relays()
+    upper, lower = scatter.total()
+    out_ref[0:32, :] = middle[0:32, :] + upper
+    out_ref[32:64, :] = middle[32:64, :] + lower
+    mail.drain()
+
+
+def layer_tail(heads_out, tokens, mlp_gain, w_out, w_gate, w_up, w_down):
+    rows_total = heads_out.shape[0]
+    bf16 = jnp.bfloat16
+    vmem = pl.BlockSpec(memory_space=pltpu.VMEM)
+    hbm = pl.BlockSpec(memory_space=pl.ANY)
+    buffers = [pltpu.VMEM(shape, bf16) for shape in SCATTER_BUFFERS]
+    copies = 2 * SCATTER_COPIES + GATHER_COPIES
+    return pl.pallas_call(
+        tail_kernel,
+        out_shape=jax.ShapeDtypeStruct(tokens.shape, jnp.float32),
+        in_specs=[vmem, vmem, vmem, hbm, hbm, hbm, hbm],
+        out_specs=vmem,
+        scratch_shapes=[
+            pltpu.VMEM(w_out.shape, bf16),
+            pltpu.VMEM((w_gate.shape[0], 2 * w_gate.shape[1]), bf16),
+            pltpu.VMEM(w_down.shape, bf16),
+            pltpu.VMEM((rows_total, WIDTH), bf16),
+            pltpu.VMEM((rows_total, WIDTH), bf16),
+            pltpu.VMEM((rows_total, WIDTH), bf16),
+            pltpu.VMEM(tokens.shape, jnp.float32),
+            *buffers,
+            *buffers,
+            pltpu.SemaphoreType.DMA((4,)),
+            pltpu.SemaphoreType.DMA((copies,)),
+            pltpu.SemaphoreType.DMA((copies,)),
+        ],
+        compiler_params=pltpu.CompilerParams(
+            collective_id=1, has_side_effects=True, vmem_limit_bytes=56 * 1024 * 1024
+        ),
+        name="layer_tail",
+    )(heads_out, tokens, mlp_gain[None, :], w_out, w_gate, w_up, w_down)
 
 
 def body(
@@ -181,9 +544,7 @@
     requests_dev = cached_length.shape[0]
     window_len = WINDOW_TOKENS
     span_len = SPAN_TOKENS
-    rows_own = tokens.shape[0]
     score_scale = 1.0 / math.sqrt(head_dim)
-    tp_index = lax.axis_index("tp")
     all_rows = lax.all_gather(tokens, "tp", axis=0, tiled=True)
     residual = all_rows.astype(jnp.float32)
     normalized_input = rms_rows(residual, attn_gain).astype(jnp.bfloat16)
@@ -242,18 +603,7 @@
         .astype(jnp.bfloat16)
         .reshape(rows_total, heads_dev * head_dim)
     )
-    attn = lax.psum(
-        jnp.dot(heads_out, w_out, preferred_element_type=jnp.float32).astype(jnp.bfloat16), "tp"
-    ).astype(jnp.float32)
-    middle = residual + attn
-    hidden = swiglu(rms_rows(middle, mlp_gain).astype(jnp.bfloat16), w_gate, w_up)
-    branch = lax.psum(
-        jnp.dot(hidden, w_down, preferred_element_type=jnp.float32).astype(jnp.bfloat16), "tp"
-    ).astype(jnp.float32)
-    row_start = tp_index * rows_own
-    output = lax.dynamic_slice_in_dim(middle, row_start, rows_own, 0) + lax.dynamic_slice_in_dim(
-        branch, row_start, rows_own, 0
-    )
+    output = layer_tail(heads_out, tokens, mlp_gain, w_out, w_gate, w_up, w_down)
     return (output, app_keys, app_values)
 
 

time: 338 us -> 212 us (0.63)
  waiting for transfers between devices: 230 us -> 48.9 us
  Pallas kernels: 0 us -> 56 us
  local copies, waits for them, and re-layouts: 19.5 us -> 30.7 us
  matrix products: 34.5 us -> 25 us
    psum x2 -> x0, waiting for transfers between devices: 176 us -> none  [the longest x1 90.2 us: body(): lax.psum(jnp.dot(heads_out, w_out, preferred_element_type=jnp.float32).as...]
    pallas_call x0 -> x1, Pallas kernels: none -> 56 us  [layer_tail(): pl.pallas_call(tail_kernel, out_shape=jax.ShapeDtypeStruct(tokens.shape,...]
    dot_general x3 -> x0, matrix products: 11.2 us -> none  [the longest x1 6.41 us: body(): jnp.dot(hidden, w_down, preferred_element_type=jnp.float32)]
    concatenate x6, local copies, waits for them, and re-layouts: 0.69 us -> 9.24 us  [rotary(): jnp.concatenate([first_half * cosine - second_half * sine_part, second_ha...]
    reduce_sum x2 -> x1, other arithmetic: 7.22 us -> 2.22 us  [rms_rows(): mean_square = jnp.mean(values * values, axis=-1, keepdims=True)]
    unnamed x48 -> x73, local copies, waits for them, and re-layouts: 9.64 us -> 11.1 us
  transfers between devices with their start and end apart: 5 -> 3, of which waited for: 4 -> 2; matrix products, arithmetic and copies ran while one was open for 9% -> 19% of each run, Pallas kernels for 0% -> 0%
where the time goes in v1:
time: 212 us; the launch traced here: 211 us
  Pallas kernels  56 us (26%)
  waiting for transfers between devices  48.9 us (23%)
  local copies, waits for them, and re-layouts  30.7 us (14%)
  matrix products  25 us (12%)
  other arithmetic  24.1 us (11%)
  between operations  14.5 us (7%)
  starting transfers between devices  11.6 us (5%)
    pallas_call x1, Pallas kernels, layer_tail(): pl.pallas_call(tail_kernel, out_shape=jax.ShapeDtypeStruct(tokens.shape,...  56 us
    all_gather x1, waiting for transfers between devices, body(): all_rows = lax.all_gather(tokens, 'tp', axis=0, tiled=True)  27.4 us
    all_to_all x1, waiting for transfers between devices, body(): lax.all_to_all(pooled_values, 'tp', split_axis=2, concat_axis=0, tiled=True)  20.8 us
    dot_general x1, matrix products, attend_whole(): jnp.einsum('rckgw,rwkd->rckgd', window_weights.astype(jnp.bfloat16), wind...  12.4 us
    unnamed x73, local copies, waits for them, and re-layouts  11.1 us
    concatenate x6, local copies, waits for them, and re-layouts, rotary(): jnp.concatenate([first_half * cosine - second_half * sine_part, second_ha...  9.24 us
    all_to_all x1, starting transfers between devices, body(): lax.all_to_all(pooled_values, 'tp', split_axis=2, concat_axis=0, tiled=True)  5.8 us
    all_to_all x1, starting transfers between devices, body(): lax.all_to_all(pooled_keys, 'tp', split_axis=2, concat_axis=0, tiled=True)  5.79 us
  transfers between devices with their start and end apart: 3, of which 2 were waited for; matrix products, arithmetic and copies ran while one was open for 19% of the time, Pallas kernels for 0%

profile of v1, /device:TPU:16, one launch (start us, length us, event | category | flops | bytes accessed | tf_op | source)
XLA Modules:
  0.0 210.9 jit_solution(11198179189015159713)
XLA Ops:
  7.9 3.2 %copy.40 = bf16[64,16,8,128]{3,1,0,2:T(8,128)(2,1)} copy(bf16[64,16,8,128]{3,2,1,0:T(8,128)(2,1)} %param.38) | data formatting | bytes 4194304 | tf_op args[14]
  11.1 5.8 %all-to-all-start.1 = ((bf16[64,16,8,128]{3,1,0,2:T(8,128)(2,1)}), bf16[64,16,8,128]{3,1,0,2:T(8,128)(2,1)S(1)}, u32[]{:S(2)}, u32[]{:S(2)}) async-start(bf16[64,16,8,128]{3,1,0,2:T(8,128)(2,1)} %copy.40), calls=%async_computation.1 | async-start | bytes 4194304 | tf_op jit(solution)/shard_map/all_to_all | solution.py:578
  18.4 3.2 %copy.37 = bf16[64,16,8,128]{3,1,0,2:T(8,128)(2,1)} copy(bf16[64,16,8,128]{3,2,1,0:T(8,128)(2,1)} %param.37) | data formatting | bytes 4194304 | tf_op args[13]
  21.6 1.2 multiply_cosine_fusion.1
  23.8 4.6 %or_and_fusion = pred[2,256,4096]{1,2,0:T(8,128)(4,1)} fusion(s32[256,4096]{0,1:T(8,128)S(1)} %iota_add_fusion, s32[2]{0:T(128)S(1)} %copy-done.29, pred[2,4096]{1,0:T(4,128)(4,1)S(1)} %get-tuple-element.19, pred[2,4096]{1,0:T(4,128)(4,1)S(1)} %get-tuple-element.18), kind=kLoop, calls=%fused_computation.12 | loop fusion | flops 6291456 | bytes 6307848 | tf_op jit(solution)/shard_map/and | solution.py:101
  28.3 20.8 %all-to-all-done.1 = bf16[64,16,8,128]{3,1,0,2:T(8,128)(2,1)S(1)} async-done(((bf16[64,16,8,128]{3,1,0,2:T(8,128)(2,1)}), bf16[64,16,8,128]{3,1,0,2:T(8,128)(2,1)S(1)}, u32[]{:S(2)}, u32[]{:S(2)}) %all-to-all-start.1) | async-done | bytes 2097184 | tf_op jit(solution)/shard_map/all_to_all | solution.py:578
  49.1 1.4 copy-done.3
  50.5 5.8 %all-to-all-start = ((bf16[64,16,8,128]{3,1,0,2:T(8,128)(2,1)}), bf16[64,16,8,128]{3,1,0,2:T(8,128)(2,1)}, u32[]{:S(2)}, u32[]{:S(2)}) async-start(bf16[64,16,8,128]{3,1,0,2:T(8,128)(2,1)} %copy.37), calls=%async_computation | async-start | bytes 4194304 | tf_op jit(solution)/shard_map/all_to_all | solution.py:577
  56.9 27.4 %all-gather.2.cloned.1.call-done = bf16[512,2048]{1,0:T(8,128)(2,1)} async-done(((bf16[64,2048]{1,0:T(8,128)(2,1)}), bf16[512,2048]{1,0:T(8,128)(2,1)}) %all-gather.2.cloned.1.call-update) | async-done | bytes 2097168 | tf_op jit(solution)/shard_map/all_gather | solution.py:548
  84.3 2.2 %fusion.9 = f32[512]{0:T(512)S(1)} fusion(bf16[512,2048]{1,0:T(8,128)(2,1)} %all-gather.2.cloned.1.call-done), kind=kLoop, calls=%fused_computation.15 | loop fusion | flops 3145216 | bytes 2099200 | tf_op jit(solution)/shard_map/reduce_sum | solution.py:20
  87.9 0.9 copy.48
  89.8 0.8 subtract_convert_fusion
  90.6 1.6 concatenate.35
  92.2 1.1 copy.36
  93.3 1.6 concatenate.34
  94.9 1.8 copy.35
  96.6 1.9 multiply_reduce_fusion.1
  98.6 1.2 fusion.36
  99.9 1.6 copy.61
  101.5 1.6 copy.60
  103.1 4.0 %gather_fusion.1 = bf16[512,16,128]{2,1,0:T(8,128)(2,1)} fusion(bf16[512,16,128]{2,1,0:T(8,128)(2,1)} %bitcast.154, s32[1024]{0:T(1024)S(1)} %pad_clamp_fusion), kind=kCustom, calls=%fused_computation.1.clone | custom fusion | bytes 4196352 | tf_op jit(solution)/shard_map/jit(_take)/gather | solution.py:583
  107.0 2.4 %convolution_convert_fusion = bf16[512,128]{1,0:T(8,128)(2,1)} fusion(bf16[512,2048]{1,0:T(8,128)(2,1)S(1)} %fusion.11, bf16[2048,128]{1,0:T(8,128)(2,1)} %param.28), kind=kOutput, calls=%fused_computation.27 | convolution fusion | flops 268500992 | bytes 2752512 | tf_op jit(solution)/shard_map/dot_general | solution.py:563
  109.5 4.0 %gather_fusion = bf16[512,16,128]{2,1,0:T(8,128)(2,1)} fusion(bf16[512,16,128]{2,1,0:T(8,128)(2,1)} %bitcast.11, s32[1024]{0:T(1024)S(1)} %pad_clamp_fusion), kind=kCustom, calls=%fused_computation.clone | custom fusion | bytes 4196352 | tf_op jit(solution)/shard_map/jit(_take)/gather | solution.py:580
  114.2 0.8 select_bitcast_fusion
  115.0 4.3 %bitcast_select_fusion.1 = (bf16[512,16,1,128]{3,1,0,2:T(8,128)(2,1)}, bf16[512,16,1,128]{3,1,0,2:T(8,128)(2,1)S(1)}) fusion(bf16[512,16,128]{2,1,0:T(8,128)(2,1)} %gather_fusion.1, pred[512]{0:T(512)(128)(4,1)S(1)} %copy-done.27, bf16[512,16,128]{2,1,0:T(8,128)(2,1)} %gather_fusion), kind=kLoop, calls=%fused_computation.19 | loop fusion | flops 2097152 | bytes 8389120 | tf_op jit(solution)/shard_map/jit(_take)/select_n | solution.py:583
  119.6 2.8 %fusion = (f32[2,256,2]{1,2,0:T(2,128)S(1)}, f32[2,4096,256,2]{2,1,3,0:T(8,128)S(1)}) fusion(pred[2,256,4096]{1,2,0:T(8,128)(4,1)S(1)} %copy-done.2, bf16[2,4096,128,1]{2,1,3,0:T(8,128)(2,1)S(1)} %bitcast.158, bf16[2,256,2,64]{3,1,2,0:T(8,128)(2,1)S(1)} %copy.36, bf16[2,256,2,64]{3,1,2,0:T(8,128)(2,1)S(1)} %copy-done.5), kind=kOutput, calls=%fused_computation.4 | convolution fusion | flops 1086848000 | bytes 21237760 | tf_op jit(solution)/shard_map/rckgd,rwkd->rckgw/dot_general | solution.py:111
  123.5 1.8 fusion.25
  125.3 4.1 %fusion.3 = f32[2,256,2]{1,2,0:T(2,128)S(1)} fusion(f32[2,4096,256,2]{2,1,3,0:T(8,128)S(1)} %get-tuple-element.29, f32[2,256,2]{1,2,0:T(2,128)S(1)} %maximum_maximum_fusion, pred[2,256,4096]{1,2,0:T(8,128)(4,1)S(1)} %copy-done.2), kind=kLoop, calls=%fused_computation.7 | loop fusion | flops 16776192 | bytes 18882560 | tf_op jit(solution)/shard_map/reduce_sum | solution.py:125
  129.4 12.4 %fusion.6 = f32[2,128,256,2]{1,2,3,0:T(8,128)} fusion(bf16[2,4096,128,1]{2,1,3,0:T(8,128)(2,1)} %bitcast.157, f32[2,4096,256,2]{2,1,3,0:T(8,128)} %copy-done.1, f32[2,256,2]{1,2,0:T(2,128)S(1)} %maximum_maximum_fusion, pred[2,256,4096]{1,2,0:T(8,128)(4,1)S(1)} %copy-done.2), kind=kOutput, calls=%fused_computation.10 | convolution fusion | flops 1090519040 | bytes 21499904 | tf_op jit(solution)/shard_map/rckgw,rwkd->rckgd/dot_general | solution.py:134
  142.0 1.6 fusion.21
  145.3 56.0 %layer_tail.1 = f32[64,2048]{1,0:T(8,128)} custom-call(bf16[512,256]{1,0:T(8,128)(2,1)} %fusion.27.heads_ref, bf16[64,2048]{1,0:T(8,128)(2,1)} %tokens_ref.1, f32[1,2048]{1,0:T(1,128)} %bitcast.164, bf16[256,2048]{1,0:T(8,128)(2,1)} %w_out_ref.1, bf16[2048,384]{1,0:T(8,128)(2,1)} %w_gate_ref.1, bf16[2048,384]{1,0:T(8,128)(2,1)} %w_up_ref.1, ...), custom_call_target="tpu_custom_call" | custom-call | tf_op jit(solution)/shard_map/layer_tail/pallas_call | solution.py:490
  202.1 1.9 copy.72
  (105 shorter events, 10.7 us)
Async XLA Ops:
  7.2 81.6 %copy-start = (bf16[2048,256]{1,0:T(8,128)(2,1)S(1)}, bf16[2048,256]{1,0:T(8,128)(2,1)}, u32[]{:S(2)}) copy-start(bf16[2048,256]{1,0:T(8,128)(2,1)} %param.26) | copy-start | bytes 3145732
  7.2 77.1 %all-gather.2.cloned.1.call-start = ((), (), s32[]{:S(2)}) async-start(), calls=%async_computation.2 | async-start | bytes 2359296 | tf_op jit(solution)/shard_map/all_gather | solution.py:548
  11.1 5.8 %copy-start.28 = (s32[2]{0:T(128)S(1)}, s32[2]{0:T(128)}, u32[]{:S(2)}) copy-start(s32[2]{0:T(128)} %param.41) | copy-start | bytes 28
  11.1 5.9 %copy-start.18 = (s32[1,512]{1,0:T(1,128)S(1)}, s32[1,512]{1,0:T(1,128)}, u32[]{:S(2)}) copy-start(s32[1,512]{1,0:T(1,128)} %param.45) | copy-start | bytes 6148
  11.1 6.5 %copy-start.23 = (s32[2]{0:T(128)S(1)}, s32[2]{0:T(128)}, u32[]{:S(2)}) copy-start(s32[2]{0:T(128)} %param.43) | copy-start | bytes 28
  11.1 6.5 %copy-start.32 = (s32[2]{0:T(128)S(1)}, s32[2]{0:T(128)}, u32[]{:S(2)}) copy-start(s32[2]{0:T(128)} %param.42) | copy-start | bytes 28
  11.1 38.0 %all-to-all-start.1 = ((bf16[64,16,8,128]{3,1,0,2:T(8,128)(2,1)}), bf16[64,16,8,128]{3,1,0,2:T(8,128)(2,1)S(1)}, u32[]{:S(2)}, u32[]{:S(2)}) async-start(bf16[64,16,8,128]{3,1,0,2:T(8,128)(2,1)} %copy.40), calls=%async_computation.1 | async-start | bytes 4194304 | tf_op jit(solution)/shard_map/all_to_all | solution.py:578
  18.3 3.2 %copy-start.20 = (f32[64]{0:T(128)}, f32[64]{0:T(128)S(1)}, u32[]{:S(2)}) copy-start(f32[64]{0:T(128)S(1)} %multiply_power_fusion) | copy-start | bytes 772
  18.3 4.5 %copy-start.29 = (s32[2]{0:T(128)S(1)}, s32[2]{0:T(128)}, u32[]{:S(2)}) copy-start(s32[2]{0:T(128)} %param.44) | copy-start | bytes 28
  18.4 4.7 %copy-start.24 = (s32[2]{0:T(128)S(1)}, s32[2]{0:T(128)}, u32[]{:S(2)}) copy-start(s32[2]{0:T(128)} %param.43) | copy-start | bytes 28
  50.5 58.9 %all-to-all-start = ((bf16[64,16,8,128]{3,1,0,2:T(8,128)(2,1)}), bf16[64,16,8,128]{3,1,0,2:T(8,128)(2,1)}, u32[]{:S(2)}, u32[]{:S(2)}) async-start(bf16[64,16,8,128]{3,1,0,2:T(8,128)(2,1)} %copy.37), calls=%async_computation | async-start | bytes 4194304 | tf_op jit(solution)/shard_map/all_to_all | solution.py:577
  56.3 30.2 %copy-start.16 = (f32[2048]{0:T(1024)S(1)}, f32[2048]{0:T(1024)}, u32[]{:S(2)}) copy-start(f32[2048]{0:T(1024)} %param.25) | copy-start | bytes 24580
  84.3 2.2 %copy-start.4 = (bf16[512,2048]{1,0:T(8,128)(2,1)S(1)}, bf16[512,2048]{1,0:T(8,128)(2,1)}, u32[]{:S(2)}) copy-start(bf16[512,2048]{1,0:T(8,128)(2,1)} %all-gather.2.cloned.1.call-done) | copy-start | bytes 6291460
  87.9 1.7 copy-start.30
  90.6 8.0 %copy-start.31 = (f32[128]{0:T(128)S(1)}, f32[128]{0:T(128)}, u32[]{:S(2)}) copy-start(f32[128]{0:T(128)} %param.31) | copy-start | bytes 1540
  93.3 5.4 %copy-start.21 = (f32[64]{0:T(128)S(1)}, f32[64]{0:T(128)}, u32[]{:S(2)}) copy-start(f32[64]{0:T(128)} %copy-done.20) | copy-start | bytes 772
  109.4 4.0 %copy-start.9 = (bf16[512,1,64]{0,2,1:T(8,128)(2,1)S(1)}, bf16[512,1,64]{0,2,1:T(8,128)(2,1)}, u32[]{:S(2)}) copy-start(bf16[512,1,64]{0,2,1:T(8,128)(2,1)} %get-tuple-element.12) | copy-start | bytes 196612
  109.4 4.0 %copy-start.10 = (bf16[512,1,64]{0,2,1:T(8,128)(2,1)S(1)}, bf16[512,1,64]{0,2,1:T(8,128)(2,1)}, u32[]{:S(2)}) copy-start(bf16[512,1,64]{0,2,1:T(8,128)(2,1)} %get-tuple-element.13) | copy-start | bytes 196612
  109.4 4.0 %copy-start.22 = (pred[512]{0:T(512)(128)(4,1)S(1)}, pred[512]{0:T(512)(128)(4,1)}, u32[]{:S(2)}) copy-start(pred[512]{0:T(512)(128)(4,1)} %lt.111) | copy-start | bytes 1540
  109.5 4.7 %copy-start.6 = (bf16[512,128]{1,0:T(8,128)(2,1)S(1)}, bf16[512,128]{1,0:T(8,128)(2,1)}, u32[]{:S(2)}) copy-start(bf16[512,128]{1,0:T(8,128)(2,1)} %convolution_convert_fusion) | copy-start | bytes 393220
  109.5 5.5 %copy-start.27 = (pred[512]{0:T(512)(128)(4,1)S(1)}, pred[512]{0:T(512)(128)(4,1)}, u32[]{:S(2)}) copy-start(pred[512]{0:T(512)(128)(4,1)} %compare_and_fusion) | copy-start | bytes 1540
  115.0 4.3 %copy-start.5 = (bf16[2,256,2,64]{3,1,2,0:T(8,128)(2,1)S(1)}, bf16[2,256,2,64]{3,1,2,0:T(8,128)(2,1)}, u32[]{:S(2)}) copy-start(bf16[2,256,2,64]{3,1,2,0:T(8,128)(2,1)} %copy.35) | copy-start | bytes 393220
  115.0 4.3 %copy-start.19 = (bf16[2,4,1,128]{3,1,2,0:T(4,128)(2,1)S(1)}, bf16[2,4,1,128]{3,1,2,0:T(4,128)(2,1)}, u32[]{:S(2)}) copy-start(bf16[2,4,1,128]{3,1,2,0:T(4,128)(2,1)} %param.39) | copy-start | bytes 6148
  115.0 4.3 %copy-start.25 = (pred[2,4]{1,0:T(4,128)(4,1)S(1)}, pred[2,4]{1,0:T(4,128)(4,1)}, u32[]{:S(2)}) copy-start(pred[2,4]{1,0:T(4,128)(4,1)} %compare_and_fusion.1) | copy-start | bytes 28
  115.0 4.6 %copy-start.2 = (pred[2,256,4096]{1,2,0:T(8,128)(4,1)S(1)}, pred[2,256,4096]{1,2,0:T(8,128)(4,1)}, u32[]{:S(2)}) copy-start(pred[2,256,4096]{1,2,0:T(8,128)(4,1)} %or_and_fusion) | copy-start | bytes 6291460
  119.6 2.8 %copy-start.14 = (bf16[512,1,64]{2,0,1:T(8,128)(2,1)S(1)}, bf16[512,1,64]{2,0,1:T(8,128)(2,1)}, u32[]{:S(2)}) copy-start(bf16[512,1,64]{2,0,1:T(8,128)(2,1)} %copy.61) | copy-start | bytes 196612
  119.6 2.8 %copy-start.15 = (bf16[512,1,64]{2,0,1:T(8,128)(2,1)S(1)}, bf16[512,1,64]{2,0,1:T(8,128)(2,1)}, u32[]{:S(2)}) copy-start(bf16[512,1,64]{2,0,1:T(8,128)(2,1)} %copy.60) | copy-start | bytes 196612
  122.4 7.0 %copy-start.1 = (f32[2,4096,256,2]{2,1,3,0:T(8,128)}, f32[2,4096,256,2]{2,1,3,0:T(8,128)S(1)}, u32[]{:S(2)}) copy-start(f32[2,4096,256,2]{2,1,3,0:T(8,128)S(1)} %get-tuple-element.29) | copy-start | bytes 50331652
  129.4 12.5 %copy-start.26 = (pred[2,4]{1,0:T(4,128)(4,1)S(1)}, pred[2,4]{1,0:T(4,128)(4,1)}, u32[]{:S(2)}) copy-start(pred[2,4]{1,0:T(4,128)(4,1)} %compare_and_fusion.1) | copy-start | bytes 28
  129.4 12.5 %copy-start.33 = (bf16[2,4,1,128]{3,1,2,0:T(4,128)(2,1)S(1)}, bf16[2,4,1,128]{3,1,2,0:T(4,128)(2,1)}, u32[]{:S(2)}) copy-start(bf16[2,4,1,128]{3,1,2,0:T(4,128)(2,1)} %param.40) | copy-start | bytes 6148
  141.9 2.1 %copy-start.8 = (f32[512,2]{1,0:T(8,128)S(1)}, f32[512,2]{1,0:T(8,128)}, u32[]{:S(2)}) copy-start(f32[512,2]{1,0:T(8,128)} %copy.48) | copy-start | bytes 12292
  145.3 56.0 %copy-start.11 = (bf16[512,1,128]{0,2,1:T(8,128)(2,1)S(1)}, bf16[512,1,128]{0,2,1:T(8,128)(2,1)}, u32[]{:S(2)}) copy-start(bf16[512,1,128]{0,2,1:T(8,128)(2,1)} %maximum_select_fusion) | copy-start | bytes 393220
  (5 other events, 5.0 us)
Sparse Core Ops, SparseCore 0:
  9.8 74.4 all-gather.1

commit v2 on v1

--- a/solution.py
+++ b/solution.py
@@ -1,7 +1,9 @@
+import functools
 import math
 
 import jax
 import jax.numpy as jnp
+import numpy as np
 from jax import lax
 from jax.experimental import pallas as pl
 from jax.experimental.pallas import tpu as pltpu
@@ -15,140 +17,10 @@
 ROPE_BASE = 1000000.0
 NEG_FILL = -1e30
 
-
-def rms_rows(values, gain):
-    mean_square = jnp.mean(values * values, axis=-1, keepdims=True)
-    return values * lax.rsqrt(mean_square + EPSILON) * gain
-
-
-def rotary(heads, positions):
-    head_width = heads.shape[-1]
-    half_width = head_width // 2
-    freqs = ROPE_BASE ** (-2.0 * jnp.arange(half_width, dtype=jnp.float32) / head_width)
-    angles = positions.astype(jnp.float32)[:, None] * freqs[None, :]
-    cosine = jnp.cos(angles)[:, None, :]
-    sine_part = jnp.sin(angles)[:, None, :]
-    first_half = heads[..., :half_width]
-    second_half = heads[..., half_width:]
-    return jnp.concatenate(
-        [
-            first_half * cosine - second_half * sine_part,
-            second_half * cosine + first_half * sine_part,
-        ],
-        axis=-1,
-    )
-
-
-def masked_max(scores, allowed):
-    return jnp.max(jnp.where(allowed, scores, NEG_FILL), axis=-1)
-
-
-def near_masks(cached, valid, sinks_used, reach, span_len, window_len, sink_len):
-    offsets = jnp.arange(span_len, dtype=jnp.int32)
-    sink_slots = jnp.arange(sink_len, dtype=jnp.int32)
-    sink_ok = (sink_slots[None, :] < sinks_used[:, None]) & (
-        sink_slots[None, :] < (cached - window_len)[:, None]
-    )
-    span_ok = (
-        (offsets[None, None, :] < valid[:, None, None])
-        & (offsets[None, None, :] <= offsets[None, :, None])
-        & (
-            (cached[:, None, None] + offsets[None, None, :] < sinks_used[:, None, None])
-            | (offsets[None, :, None] - offsets[None, None, :] <= reach[:, None, None])
-        )
-    )
-    return (sink_ok[:, None, None, None, :], span_ok[:, :, None, None, :])
-
-
-def near_scores(query_vectors, sink_key_rows, fresh_keys, score_scale):
-    sink_scores = (
-        jnp.einsum(
-            "rckgd,rskd->rckgs", query_vectors, sink_key_rows, preferred_element_type=jnp.float32
-        )
-        * score_scale
-    )
-    span_scores = (
-        jnp.einsum(
-            "rckgd,rtkd->rckgt", query_vectors, fresh_keys, preferred_element_type=jnp.float32
-        )
-        * score_scale
-    )
-    return (sink_scores, span_scores)
-
-
-def attend_whole(
-    query_vectors,
-    sink_key_rows,
-    sink_value_rows,
-    window_key_rows,
-    window_value_rows,
-    fresh_keys,
-    fresh_values,
-    cached,
-    valid,
-    sinks_used,
-    reach,
-    score_scale,
-):
-    span_len = query_vectors.shape[1]
-    window_len = window_key_rows.shape[1]
-    sink_ok, span_ok = near_masks(
-        cached, valid, sinks_used, reach, span_len, window_len, sink_key_rows.shape[1]
-    )
-    offsets = jnp.arange(span_len, dtype=jnp.int32)
-    window_slots = jnp.arange(window_len, dtype=jnp.int32)
-    key_positions = cached[:, None] - window_len + window_slots[None, :]
-    window_ok = (key_positions[:, None, :] >= 0) & (
-        (key_positions[:, None, :] < sinks_used[:, None, None])
-        | (
-            (window_len - window_slots)[None, None, :] + offsets[None, :, None]
-            <= reach[:, None, None]
-        )
-    )
-    window_ok = window_ok[:, :, None, None, :]
-    sink_scores, span_scores = near_scores(query_vectors, sink_key_rows, fresh_keys, score_scale)
-    window_scores = (
-        jnp.einsum(
-            "rckgd,rwkd->rckgw", query_vectors, window_key_rows, preferred_element_type=jnp.float32
-        )
-        * score_scale
-    )
-    highest = jnp.maximum(
-        jnp.maximum(masked_max(sink_scores, sink_ok), masked_max(window_scores, window_ok)),
-        masked_max(span_scores, span_ok),
-    )[..., None]
-    sink_weights = jnp.where(sink_ok, jnp.exp(sink_scores - highest), 0.0)
-    window_weights = jnp.where(window_ok, jnp.exp(window_scores - highest), 0.0)
-    span_weights = jnp.where(span_ok, jnp.exp(span_scores - highest), 0.0)
-    total = (
-        jnp.sum(sink_weights, axis=-1)
-        + jnp.sum(window_weights, axis=-1)
-        + jnp.sum(span_weights, axis=-1)
-    )
-    summed = jnp.einsum(
-        "rckgs,rskd->rckgd",
-        sink_weights.astype(jnp.bfloat16),
-        sink_value_rows,
-        preferred_element_type=jnp.float32,
-    )
-    summed = summed + jnp.einsum(
-        "rckgw,rwkd->rckgd",
-        window_weights.astype(jnp.bfloat16),
-        window_value_rows,
-        preferred_element_type=jnp.float32,
-    )
-    summed = summed + jnp.einsum(
-        "rckgt,rtkd->rckgd",
-        span_weights.astype(jnp.bfloat16),
-        fresh_values,
-        preferred_element_type=jnp.float32,
-    )
-    return summed / total[..., None]
-
-
 MESH = pl.DeviceIdType.MESH
 ROWS = 64
 WIDTH = 2048
+PEERS = ((1, False), (3, False), (0, True), (1, True), (3, True))
 
 
 def ring_place(shift, flip):
@@ -204,11 +76,11 @@
 
 def meet_neighbours():
     barrier = pltpu.get_barrier_semaphore()
-    for shift, flip in ((1, False), (3, False), (0, True)):
+    for shift, flip in PEERS:
         pl.semaphore_signal(
             barrier, inc=1, device_id={"tp": ring_place(shift, flip)}, device_id_type=MESH
         )
-    pl.semaphore_wait(barrier, 3)
+    pl.semaphore_wait(barrier, len(PEERS))
 
 
 def add_into(part, owner, first, count, arrived):
@@ -383,18 +255,156 @@
 GATHER_COPIES = 18
 
 
-def tail_kernel(
-    heads_ref,
+PAGE = 16
+NEAR = 384
+BLOCK = 512
+ROPE_HALF = 64
+
+
+def rope_frequencies():
+    return ROPE_BASE ** (-np.arange(ROPE_HALF) / ROPE_HALF)
+
+
+def rope_offsets():
+    angles = np.arange(SPAN_TOKENS)[:, None] * rope_frequencies()[None, :]
+    cosine, sine = np.cos(angles), np.sin(angles)
+    return (
+        np.concatenate([cosine, cosine], axis=1).astype(np.float32),
+        np.concatenate([-sine, sine], axis=1).astype(np.float32),
+    )
+
+
+def rope_bases(cached):
+    freqs = ROPE_BASE ** (-2.0 * jnp.arange(ROPE_HALF, dtype=jnp.float32) / (2 * ROPE_HALF))
+    angles = cached.astype(jnp.float32)[:, None] * freqs[None, :]
+    cosine, sine = jnp.cos(angles), jnp.sin(angles)
+    return jnp.concatenate([cosine, cosine, -sine, sine], axis=1).reshape(-1, 2 * ROPE_HALF)
+
+
+class Exchange:
+    def __init__(self, mail, tag, pages, arrived, relays, own_sem):
+        self.mail, self.tag, self.pages, self.arrived, self.relays = mail, tag, pages, arrived, relays
+        self.count = pages.shape[1]
+        me = ring_place(0, False)
+        self.own = pltpu.make_async_copy(pages.at[me], self.slot(me, 0, self.count), own_sem)
+
+    def slot(self, source, first, count):
+        return self.arrived.at[pl.ds(source * self.count + first, count)]
+
+    def start(self):
+        half = self.count // 2
+        me = ring_place(0, False)
+        for flip in (False, True):
+            target = self.pages.at[ring_place(2, flip)]
+            f = int(flip)
+            self.mail.send(
+                f"{self.tag}hr{f}", target.at[:half], self.relays.at[0, f], ring_place(1, False)
+            )
+            self.mail.send(
+                f"{self.tag}hl{f}", target.at[half:], self.relays.at[1, f], ring_place(3, False)
+            )
+        for name, shift, flip in (
+            ("xr", 1, True),
+            ("xl", 3, True),
+            ("dz", 0, True),
+            ("dr", 1, False),
+            ("dl", 3, False),
+        ):
+            target = ring_place(shift, flip)
+            self.mail.send(
+                self.tag + name, self.pages.at[target], self.slot(me, 0, self.count), target
+            )
+        self.own.start()
+
+    def relay(self):
+        half = self.count // 2
+        for flip in (False, True):
+            f = int(flip)
+            self.mail.wait(f"{self.tag}hr{f}", self.relays.at[0, f])
+            self.mail.send(
+                f"{self.tag}fr{f}",
+                self.relays.at[0, f],
+                self.slot(ring_place(3, False), 0, half),
+                ring_place(1, flip),
+            )
+            self.mail.wait(f"{self.tag}hl{f}", self.relays.at[1, f])
+            self.mail.send(
+                f"{self.tag}fl{f}",
+                self.relays.at[1, f],
+                self.slot(ring_place(1, False), half, half),
+                ring_place(3, flip),
+            )
+
+    def finish(self):
+        half = self.count // 2
+        self.own.wait()
+        for name, shift, flip in (
+            ("dr", 3, False),
+            ("dl", 1, False),
+            ("dz", 0, True),
+            ("xr", 3, True),
+            ("xl", 1, True),
+        ):
+            self.mail.wait(self.tag + name, self.slot(ring_place(shift, flip), 0, self.count))
+        for flip in (False, True):
+            f = int(flip)
+            self.mail.wait(f"{self.tag}fr{f}", self.slot(ring_place(2, flip), 0, half))
+            self.mail.wait(f"{self.tag}fl{f}", self.slot(ring_place(2, flip), half, half))
+
+
+EXCHANGE_COPIES = 13
+
+
+def layer_kernel(
+    cached_ref,
+    valid_ref,
+    sinks_ref,
+    reach_ref,
+    slot_ref,
     tokens_ref,
-    gain_ref,
+    attn_gain_ref,
+    query_gain_ref,
+    key_gain_ref,
+    mlp_gain_ref,
+    bases_ref,
+    cosine_ref,
+    sine_ref,
+    sink_keys_ref,
+    sink_values_ref,
+    pages_keys_ref,
+    pages_values_ref,
+    w_query_ref,
+    key_weight_ref,
+    value_weight_ref,
+    w_headgate_ref,
     w_out_ref,
     w_gate_ref,
     w_up_ref,
     w_down_ref,
     out_ref,
+    app_keys_ref,
+    app_values_ref,
+    w_in_vmem,
+    w_headgate_vmem,
     w_out_vmem,
     w_both_vmem,
     w_down_vmem,
+    rows_in,
+    queries,
+    near_keys,
+    near_values,
+    gates,
+    arrived_keys,
+    arrived_values,
+    relay_keys,
+    relay_values,
+    window_rows,
+    scores,
+    peaks,
+    weights,
+    totals,
+    near_sums,
+    heads,
     part_one,
     part_two,
     rows_mid,
@@ -403,35 +413,211 @@
 ):
     buffers_one, buffers_two = rest[:6], rest[6:12]
     load_sems, send_sems, recv_sems = rest[12:]
+    f32, bf16 = jnp.float32, jnp.bfloat16
     units = w_down_ref.shape[0]
+    head = key_weight_ref.shape[1]
+    wide = w_query_ref.shape[1]
+    group = wide // head
+    span = SPAN_TOKENS
+    query_rows = group * span
+    pages = WINDOW_TOKENS // PAGE
+    requests = cached_ref.shape[0]
+    scale = 1.0 / math.sqrt(head)
     loads = [
-        pltpu.make_async_copy(w_out_ref, w_out_vmem, load_sems.at[0]),
-        pltpu.make_async_copy(w_gate_ref, w_both_vmem.at[:, :units], load_sems.at[1]),
-        pltpu.make_async_copy(w_up_ref, w_both_vmem.at[:, units:], load_sems.at[2]),
-        pltpu.make_async_copy(w_down_ref, w_down_vmem, load_sems.at[3]),
+        pltpu.make_async_copy(src, dst, load_sems.at[k])
+        for k, (src, dst) in enumerate(
+            (
+                (w_query_ref, w_in_vmem.at[:, :wide]),
+                (key_weight_ref, w_in_vmem.at[:, wide : wide + head]),
+                (value_weight_ref, w_in_vmem.at[:, wide + head :]),
+                (w_headgate_ref, w_headgate_vmem),
+                (w_out_ref, w_out_vmem),
+                (w_gate_ref, w_both_vmem.at[:, :units]),
+                (w_up_ref, w_both_vmem.at[:, units:]),
+                (w_down_ref, w_down_vmem),
+            )
+        )
     ]
     for load in loads:
         load.start()
     meet_neighbours()
     mail = Mailer(send_sems, recv_sems)
     plane = lax.axis_index("tp") // 4
+    me = ring_place(0, False)
+
+    def rms(values, gain):
+        mean_square = jnp.mean(values * values, axis=-1, keepdims=True)
+        return values * lax.rsqrt(mean_square + EPSILON) * gain
+
+    rows_in[row_window(me, 0, ROWS), :] = rms(
+        tokens_ref[...].astype(f32), attn_gain_ref[...]
+    ).astype(bf16)
+    gather = Gather(mail, "n", rows_in)
+    gather.start()
+    for member in range(requests):
+        near_keys[member, span:, :] = jnp.zeros((NEAR - span, head), bf16)
+        near_values[member, span:, :] = jnp.zeros((NEAR - span, head), bf16)
+        sink_count = sink_keys_ref.shape[1]
+        near_keys[member, span : span + sink_count, :] = sink_keys_ref[member]
+        near_values[member, span : span + sink_count, :] = sink_values_ref[member]
+    gather.relay_near()
+    gather.relay_far()
+    exchange_keys = Exchange(mail, "k", pages_keys_ref, arrived_keys, relay_keys, load_sems.at[8])
+    exchange_values = Exchange(
+        mail, "v", pages_values_ref, arrived_values, relay_values, load_sems.at[9]
+    )
+    exchange_keys.start()
+    for load in loads[:4]:
+        load.wait()
+
+    def enter(flip):
+        member = 1 - plane if flip else plane
+        rows = pl.ds(pl.multiple_of(member * span, span), span)
+        normed = rows_in[rows, :]
+        mixed = jnp.dot(normed, w_in_vmem[...], preferred_element_type=f32)
+        logits = jnp.dot(normed, w_headgate_vmem[...], preferred_element_type=f32)
+        gates[rows, :] = 1.0 / (1.0 + jnp.exp(-logits))
+        base = bases_ref[pl.ds(2 * member, 2), :]
+        base_cosine, base_sine = base[0:1, :], base[1:2, :]
+        cosine = base_cosine * cosine_ref[...] - base_sine * sine_ref[...]
+        sine = base_sine * cosine_ref[...] + base_cosine * sine_ref[...]
+
+        def turn(values, gain):
+            normed_head = rms(values, gain)
+            return (
+                normed_head * cosine + pltpu.roll(normed_head, ROPE_HALF, axis=1) * sine
+            ).astype(bf16)
+
+        for part in range(group):
+            queries[member, part * span : (part + 1) * span, :] = turn(
+                mixed[:, part * head : (part + 1) * head], query_gain_ref[...]
+            )
+        fresh_keys = turn(mixed[:, wide : wide + head], key_gain_ref[...])
+        fresh_values = mixed[:, wide + head :].astype(bf16)
+        near_keys[member, :span, :] = fresh_keys
+        near_values[member, :span, :] = fresh_values
+        present = lax.broadcasted_iota(jnp.int32, (span, head), 0) < valid_ref[member]
+        app_keys_ref[rows, :] = jnp.where(present, fresh_keys, jnp.zeros_like(fresh_keys))
+        app_values_ref[rows, :] = jnp.where(present, fresh_values, jnp.zeros_like(fresh_values))
+
+    enter(False)
+    gather.finish()
+    exchange_keys.relay()
+    exchange_values.start()
+    enter(True)
+
+    def fetch(member, arrived):
+        def step(index, carry):
+            for part in range(8):
+                page = index * 8 + part
+                place = pl.ds(pl.multiple_of(page * PAGE, PAGE), PAGE)
+                window_rows[place, :] = arrived[slot_ref[member * pages + page]]
+            return carry
+
+        lax.fori_loop(0, pages // 8, step, 0)
+
+    def lane_tiles(values):
+        return [values[:, k : k + 128] for k in range(0, values.shape[1], 128)]
+
+    def score(member):
+        cached, valid = cached_ref[member], valid_ref[member]
+        sinks, reach = sinks_ref[member], reach_ref[member]
+        contract = (((1,), (1,)), ((), ()))
+        row = lax.broadcasted_iota(jnp.int32, (query_rows, NEAR), 0)
+        offset = jnp.where(row >= span, row - span, row)
+        column = lax.broadcasted_iota(jnp.int32, (query_rows, NEAR), 1)
+        sink = column - span
+        span_ok = (
+            (column < valid)
+            & (column <= offset)
+            & ((cached + column < sinks) | (offset - column <= reach))
+        )
+        sink_ok = (sink < sinks) & (sink < cached - WINDOW_TOKENS)
+        allowed = ((column < span) & span_ok) | (
+            (column >= span) & (sink < sink_keys_ref.shape[1]) & sink_ok
+        )
+        near = lax.dot_general(
+            queries[member], near_keys[member], contract, preferred_element_type=f32
+        )
+        near = jnp.where(allowed, near * scale, NEG_FILL)
+        scores[:, :NEAR] = near
+        peaks[...] = functools.reduce(jnp.maximum, lane_tiles(near))
+
+        def step(index, carry):
+            keys = window_rows[pl.ds(pl.multiple_of(index * BLOCK, BLOCK), BLOCK), :]
+            row = lax.broadcasted_iota(jnp.int32, (query_rows, BLOCK), 0)
+            offset = jnp.where(row >= span, row - span, row)
+            slot = lax.broadcasted_iota(jnp.int32, (query_rows, BLOCK), 1) + index * BLOCK
+            position = slot + (cached - WINDOW_TOKENS)
+            allowed = (position >= 0) & (
+                (position < sinks) | (WINDOW_TOKENS - slot + offset <= reach)
+            )
+            block = lax.dot_general(queries[member], keys, contract, preferred_element_type=f32)
+            block = jnp.where(allowed, block * scale, NEG_FILL)
+            scores[:, pl.ds(pl.multiple_of(NEAR + index * BLOCK, 128), BLOCK)] = block
+            peaks[...] = functools.reduce(jnp.maximum, lane_tiles(block), peaks[...])
+            return carry
+
+        lax.fori_loop(0, WINDOW_TOKENS // BLOCK, step, 0)
+        peak = jnp.max(peaks[...], axis=-1, keepdims=True)
+
+        def soften(place):
+            block = jnp.exp(scores[:, place] - peak)
+            weights[member, :, place] = block.astype(bf16)
+            return functools.reduce(jnp.add, lane_tiles(block))
+
+        peaks[...] = soften(pl.ds(0, NEAR))
+
+        def soft_step(index, carry):
+            peaks[...] += soften(pl.ds(pl.multiple_of(NEAR + index * BLOCK, 128), BLOCK))
+            return carry
+
+        lax.fori_loop(0, WINDOW_TOKENS // BLOCK, soft_step, 0)
+        totals[member] = jnp.sum(peaks[...], axis=-1, keepdims=True)
+        near_sums[member] = jnp.dot(
+            weights[member, :, :NEAR], near_values[member], preferred_element_type=f32
+        )
+
+    exchange_keys.finish()
+    fetch(0, arrived_keys)
+    score(0)
+    exchange_values.relay()
+    fetch(1, arrived_keys)
+    score(1)
+    exchange_values.finish()
+
+    def mix(flip):
+        member = 1 - plane if flip else plane
+        fetch(member, arrived_values)
+        summed = near_sums[member] + jnp.dot(
+            weights[member, :, NEAR:], window_rows[...], preferred_element_type=f32
+        )
+        mixture = summed / totals[member]
+        rows = pl.ds(pl.multiple_of(member * span, span), span)
+        for part in range(group):
+            heads[rows, part * head : (part + 1) * head] = (
+                mixture[part * span : (part + 1) * span, :] * gates[rows, part : part + 1]
+            ).astype(bf16)
+
     half_rows = 4 * ROWS
 
     def half(flip):
         return pl.ds(pl.multiple_of((1 - plane if flip else plane) * half_rows, half_rows), half_rows)
 
     scatter = Scatter(mail, "a", part_one, *buffers_one)
-    loads[0].wait()
+    loads[4].wait()
 
     def project(flip):
         rows = half(flip)
         part_one[rows, :] = jnp.dot(
-            heads_ref[rows, :], w_out_vmem[...], preferred_element_type=jnp.float32
-        ).astype(jnp.bfloat16)
-
+            heads[rows, :], w_out_vmem[...], preferred_element_type=f32
+        ).astype(bf16)
+
+    mix(True)
     project(True)
     scatter.start_z()
     scatter.start_x(True)
+    mix(False)
     project(False)
     scatter.start_x(False)
     scatter.relay_x(True)
@@ -439,18 +625,17 @@
     scatter.relay_z()
     scatter.finish_relays()
     upper, lower = scatter.total()
-    me = ring_place(0, False)
     for first, attn in ((0, upper), (32, lower)):
         mid = tokens_ref[first : first + 32, :].astype(jnp.float32) + attn
         middle[first : first + 32, :] = mid
         mean_square = jnp.mean(mid * mid, axis=-1, keepdims=True)
         rows_mid[row_window(me, first, 32), :] = (
-            mid * lax.rsqrt(mean_square + EPSILON) * gain_ref[...]
+            mid * lax.rsqrt(mean_square + EPSILON) * mlp_gain_ref[...]
         ).astype(jnp.bfloat16)
     gather = Gather(mail, "g", rows_mid)
     gather.start()
     gather.relay_near()
-    for load in loads[1:]:
+    for load in loads[5:]:
         load.wait()
 
     def feed(flip):
@@ -480,37 +665,115 @@
     mail.drain()
 
 
-def layer_tail(heads_out, tokens, mlp_gain, w_out, w_gate, w_up, w_down):
-    rows_total = heads_out.shape[0]
-    bf16 = jnp.bfloat16
+def layer(
+    tokens,
+    attn_gain,
+    query_gain,
+    key_gain,
+    mlp_gain,
+    sink_keys,
+    sink_values,
+    pages_keys,
+    pages_values,
+    w_query,
+    key_weight,
+    value_weight,
+    w_headgate,
+    w_out,
+    w_gate,
+    w_up,
+    w_down,
+    cached,
+    valid,
+    sinks,
+    reach,
+    slots,
+):
+    bf16, f32 = jnp.bfloat16, jnp.float32
+    requests, _, head = sink_keys.shape
+    rows_total = requests * SPAN_TOKENS
+    group = w_query.shape[1] // head
+    query_rows = group * SPAN_TOKENS
+    smem = pl.BlockSpec(memory_space=pltpu.SMEM)
     vmem = pl.BlockSpec(memory_space=pltpu.VMEM)
     hbm = pl.BlockSpec(memory_space=pl.ANY)
+    arrived = (pages_keys.shape[0] * pages_keys.shape[1], PAGE, head)
+    relays = (2, 2, pages_keys.shape[1] // 2, PAGE, head)
     buffers = [pltpu.VMEM(shape, bf16) for shape in SCATTER_BUFFERS]
-    copies = 2 * SCATTER_COPIES + GATHER_COPIES
+    copies = 2 * (SCATTER_COPIES + GATHER_COPIES + EXCHANGE_COPIES)
+    cosine, sine = rope_offsets()
     return pl.pallas_call(
-        tail_kernel,
-        out_shape=jax.ShapeDtypeStruct(tokens.shape, jnp.float32),
-        in_specs=[vmem, vmem, vmem, hbm, hbm, hbm, hbm],
-        out_specs=vmem,
+        layer_kernel,
+        out_shape=(
+            jax.ShapeDtypeStruct(tokens.shape, f32),
+            jax.ShapeDtypeStruct((rows_total, head), bf16),
+            jax.ShapeDtypeStruct((rows_total, head), bf16),
+        ),
+        in_specs=[smem] * 5 + [vmem] * 10 + [hbm] * 10,
+        out_specs=(vmem, vmem, vmem),
         scratch_shapes=[
+            pltpu.VMEM((w_query.shape[0], (group + 2) * head), bf16),
+            pltpu.VMEM(w_headgate.shape, bf16),
             pltpu.VMEM(w_out.shape, bf16),
             pltpu.VMEM((w_gate.shape[0], 2 * w_gate.shape[1]), bf16),
             pltpu.VMEM(w_down.shape, bf16),
             pltpu.VMEM((rows_total, WIDTH), bf16),
+            pltpu.VMEM((requests, query_rows, head), bf16),
+            pltpu.VMEM((requests, NEAR, head), bf16),
+            pltpu.VMEM((requests, NEAR, head), bf16),
+            pltpu.VMEM((rows_total, w_headgate.shape[1]), f32),
+            pltpu.VMEM(arrived, bf16),
+            pltpu.VMEM(arrived, bf16),
+            pltpu.VMEM(relays, bf16),
+            pltpu.VMEM(relays, bf16),
+            pltpu.VMEM((WINDOW_TOKENS, head), bf16),
+            pltpu.VMEM((query_rows, NEAR + WINDOW_TOKENS), f32),
+            pltpu.VMEM((query_rows, 128), f32),
+            pltpu.VMEM((requests, query_rows, NEAR + WINDOW_TOKENS), bf16),
+            pltpu.VMEM((requests, query_rows, 1), f32),
+            pltpu.VMEM((requests, query_rows, head), f32),
+            pltpu.VMEM((rows_total, group * head), bf16),
             pltpu.VMEM((rows_total, WIDTH), bf16),
             pltpu.VMEM((rows_total, WIDTH), bf16),
-            pltpu.VMEM(tokens.shape, jnp.float32),
+            pltpu.VMEM((rows_total, WIDTH), bf16),
+            pltpu.VMEM(tokens.shape, f32),
             *buffers,
             *buffers,
-            pltpu.SemaphoreType.DMA((4,)),
+            pltpu.SemaphoreType.DMA((10,)),
             pltpu.SemaphoreType.DMA((copies,)),
             pltpu.SemaphoreType.DMA((copies,)),
         ],
         compiler_params=pltpu.CompilerParams(
-            collective_id=1, has_side_effects=True, vmem_limit_bytes=56 * 1024 * 1024
+            collective_id=1, has_side_effects=True, vmem_limit_bytes=63 * 1024 * 1024
         ),
-        name="layer_tail",
-    )(heads_out, tokens, mlp_gain[None, :], w_out, w_gate, w_up, w_down)
+        name="layer",
+    )(
+        cached,
+        valid,
+        sinks,
+        reach,
+        slots,
+        tokens,
+        attn_gain[None, :],
+        query_gain[None, :],
+        key_gain[None, :],
+        mlp_gain[None, :],
+        rope_bases(cached),
+        jnp.asarray(cosine),
+        jnp.asarray(sine),
+        sink_keys,
+        sink_values,
+        pages_keys,
+        pages_values,
+        w_query,
+        key_weight,
+        value_weight,
+        w_headgate,
+        w_out,
+        w_gate,
+        w_up,
+        w_down,
+    )
 
 
 def body(
@@ -538,73 +801,35 @@
     page_slot,
 ):
     head_dim = query_gain.shape[0]
-    heads_dev = w_query.shape[1] // head_dim
-    kv_dev = key_weight.shape[1] // head_dim
-    group_size = heads_dev // kv_dev
-    requests_dev = cached_length.shape[0]
-    window_len = WINDOW_TOKENS
-    span_len = SPAN_TOKENS
-    score_scale = 1.0 / math.sqrt(head_dim)
-    all_rows = lax.all_gather(tokens, "tp", axis=0, tiled=True)
-    residual = all_rows.astype(jnp.float32)
-    normalized_input = rms_rows(residual, attn_gain).astype(jnp.bfloat16)
-    rows_total = normalized_input.shape[0]
-    offsets = jnp.arange(span_len, dtype=jnp.int32)
-    positions = (cached_length[:, None] + offsets[None, :]).reshape(rows_total)
-    query_vectors = jnp.dot(normalized_input, w_query, preferred_element_type=jnp.float32).reshape(
-        rows_total, heads_dev, head_dim
-    )
-    query_vectors = rotary(rms_rows(query_vectors, query_gain), positions).astype(jnp.bfloat16)
-    fresh_keys = jnp.dot(normalized_input, key_weight, preferred_element_type=jnp.float32).reshape(
-        rows_total, kv_dev, head_dim
-    )
-    fresh_keys = rotary(rms_rows(fresh_keys, key_gain), positions).astype(jnp.bfloat16)
-    fresh_values = (
-        jnp.dot(normalized_input, value_weight, preferred_element_type=jnp.float32)
-        .astype(jnp.bfloat16)
-        .reshape(rows_total, kv_dev, head_dim)
-    )
-    headgate = jax.nn.sigmoid(
-        jnp.dot(normalized_input, w_headgate, preferred_element_type=jnp.float32)
-    )
-    present = (offsets[None, :] < valid_length[:, None]).reshape(rows_total)[:, None, None]
-    app_keys = jnp.where(present, fresh_keys, jnp.zeros_like(fresh_keys))
-    app_values = jnp.where(present, fresh_values, jnp.zeros_like(fresh_values))
-    query_blocks = query_vectors.reshape(requests_dev, span_len, kv_dev, group_size, head_dim)
-    key_blocks = fresh_keys.reshape(requests_dev, span_len, kv_dev, head_dim)
-    value_blocks = fresh_values.reshape(requests_dev, span_len, kv_dev, head_dim)
-    arrived_keys, arrived_values = (
-        lax.all_to_all(pooled_keys, "tp", split_axis=2, concat_axis=0, tiled=True),
-        lax.all_to_all(pooled_values, "tp", split_axis=2, concat_axis=0, tiled=True),
-    )
-    window_key_rows = jnp.take(arrived_keys, page_slot[0], axis=0).reshape(
-        requests_dev, window_len, kv_dev, head_dim
-    )
-    window_value_rows = jnp.take(arrived_values, page_slot[0], axis=0).reshape(
-        requests_dev, window_len, kv_dev, head_dim
-    )
-    mixture = attend_whole(
-        query_blocks,
-        sink_key_cache,
-        sink_value_cache,
-        window_key_rows,
-        window_value_rows,
-        key_blocks,
-        value_blocks,
+
+    def by_head(pool):
+        return pool.transpose(2, 0, 1, 3)
+
+    output, app_keys, app_values = layer(
+        tokens,
+        attn_gain,
+        query_gain,
+        key_gain,
+        mlp_gain,
+        sink_key_cache[:, :, 0, :],
+        sink_value_cache[:, :, 0, :],
+        by_head(pooled_keys),
+        by_head(pooled_values),
+        w_query,
+        key_weight,
+        value_weight,
+        jnp.pad(w_headgate, ((0, 0), (0, 128 - w_headgate.shape[1]))),
+        w_out,
+        w_gate,
+        w_up,
+        w_down,
         cached_length,
         valid_length,
         sink_position_count,
         window,
-        score_scale,
+        page_slot[0],
     )
-    mixture = mixture.reshape(rows_total, heads_dev, head_dim)
-    heads_out = (
-        (mixture * headgate[..., None])
-        .astype(jnp.bfloat16)
-        .reshape(rows_total, heads_dev * head_dim)
-    )
-    output = layer_tail(heads_out, tokens, mlp_gain, w_out, w_gate, w_up, w_down)
-    return (output, app_keys, app_values)
+    return (output, app_keys[:, None, :], app_values[:, None, :])
 
 
 def solution(mesh):

time: 212 us -> 136 us (0.64)
  Pallas kernels: 56 us -> 122 us
  waiting for transfers between devices: 48.9 us -> 0 us
  matrix products: 25 us -> 0 us
  other arithmetic: 24.1 us -> 0.86 us
  local copies, waits for them, and re-layouts: 30.7 us -> 12.4 us
  between operations: 14.5 us -> 0.65 us
  starting transfers between devices: 11.6 us -> 0 us
    pallas_call x1, Pallas kernels: 56 us -> 122 us  [layer(): pl.pallas_call(layer_kernel, out_shape=(jax.ShapeDtypeStruct(tokens.shape...]
    all_gather x1 -> x0, waiting for transfers between devices: 27.4 us -> none  [body(): all_rows = lax.all_gather(tokens, 'tp', axis=0, tiled=True)]
    dot_general x10 -> x0, matrix products: 25 us -> none  [the longest x1 12.4 us: attend_whole(): jnp.einsum('rckgw,rwkd->rckgd', window_weights.astype(jnp.bfloat16), wind...]
    all_to_all x2 -> x0, waiting for transfers between devices: 20.8 us -> none  [the longest x1 20.8 us: body(): lax.all_to_all(pooled_values, 'tp', split_axis=2, concat_axis=0, tiled=True)]
    all_to_all x2 -> x0, starting transfers between devices: 11.6 us -> none  [the longest x1 5.8 us: body(): lax.all_to_all(pooled_values, 'tp', split_axis=2, concat_axis=0, tiled=True)]
    concatenate x6 -> x0, local copies, waits for them, and re-layouts: 9.24 us -> none  [rotary(): jnp.concatenate([first_half * cosine - second_half * sine_part, second_ha...]
    gather x2 -> x0, local copies, waits for them, and re-layouts: 7.96 us -> none  [the longest x1 3.99 us: body(): jnp.take(arrived_keys, page_slot[0], axis=0)]
    reduce_sum x4 -> x0, other arithmetic: 6.66 us -> none  [the longest x1 4.11 us: attend_whole(): jnp.sum(window_weights, axis=-1)]
  transfers between devices with their start and end apart: 3 -> 0, of which waited for: 2 -> 0; matrix products, arithmetic and copies ran while one was open for 19% -> 0% of each run, Pallas kernels for 0% -> 0%
where the time goes in v2:
time: 136 us
  Pallas kernels  122 us (90%)
  local copies, waits for them, and re-layouts  12.4 us (9%)
    pallas_call x1, Pallas kernels, layer(): pl.pallas_call(layer_kernel, out_shape=(jax.ShapeDtypeStruct(tokens.shape...  122 us
    unnamed x4, local copies, waits for them, and re-layouts  6.01 us
    transpose x1, local copies, waits for them, and re-layouts, by_head(): return pool.transpose(2, 0, 1, 3)  4.9 us

profile of v2, /device:TPU:16, one launch (start us, length us, event | category | flops | bytes accessed | tf_op | source)
XLA Modules:
  0.0 136.1 jit_solution(18192929086493172308)
XLA Ops:
  0.6 0.7 convert_element_type.5
  1.3 0.1 multiply_cosine_fusion
  1.4 0.1 pad_maximum_fusion
  1.5 0.6 reshape.15.bases_ref
  2.1 1.0 copy.29
  3.1 0.9 pad.4.w_headgate_ref
  4.0 4.9 %copy_bitcast_fusion = (bf16[8,64,16,128]{3,2,1,0:T(8,128)(2,1)}, bf16[8,64,16,128]{3,2,1,0:T(8,128)(2,1)}) fusion(bf16[64,16,8,128]{3,2,1,0:T(8,128)(2,1)} %param.38, bf16[64,16,8,128]{3,2,1,0:T(8,128)(2,1)} %param.37), kind=kLoop, calls=%fused_computation | loop fusion | bytes 8388608 | tf_op jit(solution)/shard_map/transpose | solution.py:806
  8.9 122.1 %layer.1 = (f32[64,2048]{1,0:T(8,128)}, bf16[512,128]{1,0:T(8,128)(2,1)}, bf16[512,128]{1,0:T(8,128)(2,1)}) custom-call(s32[2]{0:T(128)} %cached_ref.1, s32[2]{0:T(128)} %valid_ref.1, s32[2]{0:T(128)} %sinks_ref.1, s32[2]{0:T(128)} %reach_ref.1, s32[512]{0:T(512)} %bitcast.17, bf16[64,2048]{1,0:T(8,128)(2,1)} %tokens_ref.1, f32[1,2048]{1,0:T(1,128)} %bitcast.15, ...), custom_call_target="tpu_custom_call" | custom-call | tf_op jit(solution)/shard_map/layer/pallas_call | solution.py:705
  131.0 1.9 %copy.35 = f32[64,2048]{1,0:T(8,128)} copy(f32[64,2048]{1,0:T(8,128)} %get-tuple-element.17) | data formatting | bytes 1048576
  132.9 1.6 %copy.36 = bf16[512,1,128]{2,0,1:T(8,128)(2,1)} copy(bf16[512,1,128]{2,0,1:T(8,128)(2,1)} %bitcast.14) | data formatting | bytes 262144
  134.5 1.6 %copy.37 = bf16[512,1,128]{2,0,1:T(8,128)(2,1)} copy(bf16[512,1,128]{2,0,1:T(8,128)(2,1)} %bitcast.13) | data formatting | bytes 262144
  (1 shorter events, 0.0 us)

commit v3 on v2

--- a/solution.py
+++ b/solution.py
@@ -21,6 +21,8 @@
 ROWS = 64
 WIDTH = 2048
 PEERS = ((1, False), (3, False), (0, True), (1, True), (3, True))
+CORES = 2
+Z_GROUPS = 4
 
 
 def ring_place(shift, flip):
@@ -29,6 +31,16 @@
     z = t // 4
     plane = 1 - z if flip else z
     return lax.rem(x + shift, 4) + 4 * plane
+
+
+def beyond_place():
+    req = lax.axis_index("req")
+    t = lax.axis_index("tp")
+    group = req // CORES
+    z_group = lax.rem(group, Z_GROUPS)
+    step = jnp.where(t // 4 == 1, 1, Z_GROUPS - 1)
+    moved = group - z_group + lax.rem(z_group + step, Z_GROUPS)
+    return {"req": moved * CORES + lax.rem(req, CORES), "tp": ring_place(0, True)}
 
 
 def row_window(owner, first, count):
@@ -51,7 +63,7 @@
             dst_ref=dst,
             send_sem=self.send_sems.at[k],
             recv_sem=self.recv_sems.at[k],
-            device_id={"tp": target},
+            device_id=target if isinstance(target, dict) else {"tp": target},
             device_id_type=MESH,
         )
         copy.start()
@@ -80,7 +92,8 @@
         pl.semaphore_signal(
             barrier, inc=1, device_id={"tp": ring_place(shift, flip)}, device_id_type=MESH
         )
-    pl.semaphore_wait(barrier, len(PEERS))
+    pl.semaphore_signal(barrier, inc=1, device_id=beyond_place(), device_id_type=MESH)
+    pl.semaphore_wait(barrier, len(PEERS) + 1)
 
 
 def add_into(part, owner, first, count, arrived):
@@ -113,7 +126,7 @@
         self.put(f"h2l{f}0", self.rows(3, flip, 0, 16), self.h2.at[1, f, 0], self.left)
 
     def start_z(self):
-        for k, shift in enumerate((2, 1, 3, 0)):
+        for k, shift in enumerate((2, 1, 3)):
             self.put(f"zb{k}", self.rows(shift, True, 32, 32), self.zb.at[k], self.across)
 
     def relay_x(self, flip):
@@ -137,7 +150,7 @@
         add_into(self.part, ring_place(3, False), 32, 32, self.zb.at[2])
         self.put("b2l0", self.rows(3, False, 32, 16), self.b2.at[1, 0], self.left)
 
-    def finish_relays(self):
+    def cross(self):
         for side, letter in ((0, "r"), (1, "l")):
             for half in (0, 1):
                 self.got(f"h2{letter}1{half}", self.h2.at[side, 1, half])
@@ -148,6 +161,9 @@
             + self.h2[1, 1].reshape(32, WIDTH).astype(jnp.float32)
         ).astype(jnp.bfloat16)
         self.put("za", self.rows(0, True, 0, 32), self.za, self.across)
+        self.put("zb3", self.rows(0, True, 32, 32), self.zb.at[3], self.across)
+
+    def finish_relays(self):
         self.got("b1r", self.b1.at[0])
         add_into(self.part, ring_place(1, False), 32, 16, self.b1.at[0])
         self.put("b2r0", self.rows(1, False, 32, 16), self.b2.at[0, 0], self.right)
@@ -155,30 +171,31 @@
         add_into(self.part, ring_place(3, False), 48, 16, self.b1.at[1])
         self.put("b2l1", self.rows(3, False, 48, 16), self.b2.at[1, 1], self.left)
 
-    def total(self):
-        me = ring_place(0, False)
+    def upper(self):
         f32 = jnp.float32
         for side, letter in ((0, "r"), (1, "l")):
             for half in (0, 1):
                 self.got(f"h2{letter}0{half}", self.h2.at[side, 0, half])
         upper = (
-            self.part[row_window(me, 0, 32), :].astype(f32)
+            self.part[row_window(ring_place(0, False), 0, 32), :].astype(f32)
             + self.h2[0, 0].reshape(32, WIDTH).astype(f32)
             + self.h2[1, 0].reshape(32, WIDTH).astype(f32)
         )
-        self.got("zb3", self.zb.at[3])
-        lower = self.part[row_window(me, 32, 32), :].astype(f32) + self.zb[3].astype(f32)
+        self.got("za", self.za)
+        return upper + self.za[...].astype(f32)
+
+    def lower(self):
+        f32 = jnp.float32
         for side, letter in ((0, "r"), (1, "l")):
             for half in (0, 1):
                 self.got(f"b2{letter}{half}", self.b2.at[side, half])
-        lower = (
-            lower
+        self.got("zb3", self.zb.at[3])
+        return (
+            self.part[row_window(ring_place(0, False), 32, 32), :].astype(f32)
             + self.b2[0].reshape(32, WIDTH).astype(f32)
             + self.b2[1].reshape(32, WIDTH).astype(f32)
-        )
-        self.got("za", self.za)
-        upper = upper + self.za[...].astype(f32)
-        return upper, lower
+            + self.zb[3].astype(f32)
+        )
 
 
 SCATTER_BUFFERS = [
@@ -253,6 +270,128 @@
 
 
 GATHER_COPIES = 18
+OWN_ROWS = 4 * ROWS
+HALF = ROWS // 2
+
+
+def x_place(shift):
+    return lax.rem(lax.axis_index("tp") + shift, 4)
+
+
+def wide_window(block, shift, half=None):
+    x = x_place(shift)
+    if block == 0:
+        return pl.ds(pl.multiple_of(x * ROWS + (half or 0) * HALF, HALF), ROWS if half is None else HALF)
+    return pl.ds(pl.multiple_of(OWN_ROWS + (block - 1) * 4 * HALF + x * HALF, HALF), HALF)
+
+
+class WideGather:
+    def __init__(self, mail, rows):
+        self.mail, self.rows = mail, rows
+        self.right, self.left = ring_place(1, False), ring_place(3, False)
+        self.over = (ring_place(0, True), beyond_place())
+
+    def put(self, name, shift, half, block, target):
+        self.mail.send(
+            "w" + name,
+            self.rows.at[wide_window(0, shift, half), :],
+            self.rows.at[wide_window(block, shift, half), :],
+            target,
+        )
+
+    def got(self, name, shift, half, block):
+        self.mail.wait("w" + name, self.rows.at[wide_window(block, shift, half), :])
+
+    def start(self, half):
+        self.put(f"r{half}", 0, half, 0, self.right)
+        self.put(f"l{half}", 0, half, 0, self.left)
+        self.put(f"z{half}0", 0, half, half + 1, self.over[half])
+
+    def relay(self):
+        for half in (0, 1):
+            self.got(f"r{half}", 3, half, 0)
+            if half == 0:
+                self.put("rr", 3, half, 0, self.right)
+            self.put(f"z{half}3", 3, half, half + 1, self.over[half])
+            self.got(f"l{half}", 1, half, 0)
+            if half == 1:
+                self.put("ll", 1, half, 0, self.left)
+            self.put(f"z{half}1", 1, half, half + 1, self.over[half])
+        self.got("rr", 2, 0, 0)
+        self.put("z02", 2, 0, 1, self.over[0])
+        self.got("ll", 2, 1, 0)
+        self.put("z12", 2, 1, 2, self.over[1])
+
+    def finish(self, half):
+        for shift in (0, 3, 1, 2):
+            self.got(f"z{half}{shift}", shift, half, half + 1)
+
+
+WIDE_GATHER_COPIES = 14
+
+
+class WideScatter:
+    def __init__(self, mail, part, arrived, hop_one, hop_two):
+        self.mail, self.part, self.arrived = mail, part, arrived
+        self.hop_one, self.hop_two = hop_one, hop_two
+        self.right, self.left = ring_place(1, False), ring_place(3, False)
+        self.over = (ring_place(0, True), beyond_place())
+
+    def start(self, half):
+        for k, shift in enumerate((2, 1, 3, 0)):
+            self.mail.send(
+                f"y{half}{k}",
+                self.part.at[wide_window(half + 1, shift), :],
+                self.arrived.at[half, k],
+                self.over[half],
+            )
+
+    def fold(self, half, k, shift):
+        self.mail.wait(f"y{half}{k}", self.arrived.at[half, k])
+        self.add(shift, half, self.arrived[half, k])
+
+    def add(self, shift, half, values):
+        rows = wide_window(0, shift, half)
+        self.part[rows, :] = (
+            self.part[rows, :].astype(jnp.float32) + values.astype(jnp.float32)
+        ).astype(jnp.bfloat16)
+
+    def put(self, name, shift, half, dst, target):
+        self.mail.send("y" + name, self.part.at[wide_window(0, shift, half), :], dst, target)
+
+    def relay(self):
+        self.fold(0, 0, 2)
+        self.put("hr", 2, 0, self.hop_one.at[0], self.right)
+        self.fold(1, 0, 2)
+        self.put("hl", 2, 1, self.hop_one.at[1], self.left)
+        self.fold(1, 1, 1)
+        self.put("r1", 1, 1, self.hop_two.at[0, 1], self.right)
+        self.fold(0, 1, 1)
+        self.mail.wait("yhr", self.hop_one.at[0])
+        self.add(1, 0, self.hop_one[0])
+        self.put("r0", 1, 0, self.hop_two.at[0, 0], self.right)
+        self.fold(0, 2, 3)
+        self.put("l0", 3, 0, self.hop_two.at[1, 0], self.left)
+        self.fold(1, 2, 3)
+        self.mail.wait("yhl", self.hop_one.at[1])
+        self.add(3, 1, self.hop_one[1])
+        self.put("l1", 3, 1, self.hop_two.at[1, 1], self.left)
+
+    def total(self, half):
+        f32 = jnp.float32
+        self.mail.wait(f"y{half}3", self.arrived.at[half, 3])
+        self.mail.wait(f"yr{half}", self.hop_two.at[0, half])
+        self.mail.wait(f"yl{half}", self.hop_two.at[1, half])
+        return (
+            self.part[wide_window(0, 0, half), :].astype(f32)
+            + self.arrived[half, 3].astype(f32)
+            + self.hop_two[0, half].astype(f32)
+            + self.hop_two[1, half].astype(f32)
+        )
+
+
+WIDE_BUFFERS = [(2, 4, HALF, WIDTH), (2, HALF, WIDTH), (2, 2, HALF, WIDTH)]
+WIDE_SCATTER_COPIES = 14
 
 
 PAGE = 16
@@ -272,13 +411,6 @@
         np.concatenate([cosine, cosine], axis=1).astype(np.float32),
         np.concatenate([-sine, sine], axis=1).astype(np.float32),
     )
-
-
-def rope_bases(cached):
-    freqs = ROPE_BASE ** (-2.0 * jnp.arange(ROPE_HALF, dtype=jnp.float32) / (2 * ROPE_HALF))
-    angles = cached.astype(jnp.float32)[:, None] * freqs[None, :]
-    cosine, sine = jnp.cos(angles), jnp.sin(angles)
-    return jnp.concatenate([cosine, cosine, -sine, sine], axis=1).reshape(-1, 2 * ROPE_HALF)
 
 
 class Exchange:
@@ -366,7 +498,7 @@
     query_gain_ref,
     key_gain_ref,
     mlp_gain_ref,
-    bases_ref,
+    freqs_ref,
     cosine_ref,
     sine_ref,
     sink_keys_ref,
@@ -382,8 +514,8 @@
     w_up_ref,
     w_down_ref,
     out_ref,
-    app_keys_ref,
-    app_values_ref,
+    fresh_keys_ref,
+    fresh_values_ref,
     w_in_vmem,
     w_headgate_vmem,
     w_out_vmem,
@@ -396,6 +528,9 @@
     gates,
     arrived_keys,
     arrived_values,
+    raw_pages,
+    head_keys,
+    head_values,
     relay_keys,
     relay_values,
     window_rows,
@@ -411,13 +546,13 @@
     middle,
     *rest,
 ):
-    buffers_one, buffers_two = rest[:6], rest[6:12]
-    load_sems, send_sems, recv_sems = rest[12:]
+    buffers_one, buffers_two = rest[:6], rest[6:9]
+    load_sems, send_sems, recv_sems = rest[9:]
     f32, bf16 = jnp.float32, jnp.bfloat16
     units = w_down_ref.shape[0]
     head = key_weight_ref.shape[1]
-    wide = w_query_ref.shape[1]
-    group = wide // head
+    query_width = w_query_ref.shape[1]
+    group = query_width // head
     span = SPAN_TOKENS
     query_rows = group * span
     pages = WINDOW_TOKENS // PAGE
@@ -427,9 +562,9 @@
         pltpu.make_async_copy(src, dst, load_sems.at[k])
         for k, (src, dst) in enumerate(
             (
-                (w_query_ref, w_in_vmem.at[:, :wide]),
-                (key_weight_ref, w_in_vmem.at[:, wide : wide + head]),
-                (value_weight_ref, w_in_vmem.at[:, wide + head :]),
+                (w_query_ref, w_in_vmem.at[:, :query_width]),
+                (key_weight_ref, w_in_vmem.at[:, query_width : query_width + head]),
+                (value_weight_ref, w_in_vmem.at[:, query_width + head :]),
                 (w_headgate_ref, w_headgate_vmem),
                 (w_out_ref, w_out_vmem),
                 (w_gate_ref, w_both_vmem.at[:, :units]),
@@ -438,7 +573,11 @@
             )
         )
     ]
-    for load in loads:
+    raw_loads = [
+        pltpu.make_async_copy(pages_keys_ref, raw_pages.at[0], load_sems.at[10]),
+        pltpu.make_async_copy(pages_values_ref, raw_pages.at[1], load_sems.at[11]),
+    ]
+    for load in raw_loads + loads:
         load.start()
     meet_neighbours()
     mail = Mailer(send_sems, recv_sems)
@@ -460,11 +599,25 @@
         sink_count = sink_keys_ref.shape[1]
         near_keys[member, span : span + sink_count, :] = sink_keys_ref[member]
         near_values[member, span : span + sink_count, :] = sink_values_ref[member]
+
+    def by_head(which, target):
+        raw_loads[which].wait()
+        count = 8
+
+        def step(index, carry):
+            place = pl.ds(index * count, count)
+            block = raw_pages[which, place].reshape(count * PAGE, *raw_pages.shape[3:])
+            target[:, place] = jnp.swapaxes(block, 0, 1).reshape(-1, count, PAGE, head)
+            return carry
+
+        lax.fori_loop(0, raw_pages.shape[1] // count, step, 0)
+
+    by_head(0, head_keys)
     gather.relay_near()
     gather.relay_far()
-    exchange_keys = Exchange(mail, "k", pages_keys_ref, arrived_keys, relay_keys, load_sems.at[8])
+    exchange_keys = Exchange(mail, "k", head_keys, arrived_keys, relay_keys, load_sems.at[8])
     exchange_values = Exchange(
-        mail, "v", pages_values_ref, arrived_values, relay_values, load_sems.at[9]
+        mail, "v", head_values, arrived_values, relay_values, load_sems.at[9]
     )
     exchange_keys.start()
     for load in loads[:4]:
@@ -475,10 +628,14 @@
         rows = pl.ds(pl.multiple_of(member * span, span), span)
         normed = rows_in[rows, :]
         mixed = jnp.dot(normed, w_in_vmem[...], preferred_element_type=f32)
-        logits = jnp.dot(normed, w_headgate_vmem[...], preferred_element_type=f32)
+        logits = lax.dot_general(
+            normed, w_headgate_vmem[...], (((1,), (1,)), ((), ())), preferred_element_type=f32
+        )
         gates[rows, :] = 1.0 / (1.0 + jnp.exp(-logits))
-        base = bases_ref[pl.ds(2 * member, 2), :]
-        base_cosine, base_sine = base[0:1, :], base[1:2, :]
+        angles = cached_ref[member].astype(f32) * freqs_ref[...]
+        lanes = lax.broadcasted_iota(jnp.int32, angles.shape, 1)
+        base_cosine = jnp.cos(angles)
+        base_sine = jnp.where(lanes < ROPE_HALF, -jnp.sin(angles), jnp.sin(angles))
         cosine = base_cosine * cosine_ref[...] - base_sine * sine_ref[...]
         sine = base_sine * cosine_ref[...] + base_cosine * sine_ref[...]
 
@@ -492,14 +649,14 @@
             queries[member, part * span : (part + 1) * span, :] = turn(
                 mixed[:, part * head : (part + 1) * head], query_gain_ref[...]
             )
-        fresh_keys = turn(mixed[:, wide : wide + head], key_gain_ref[...])
-        fresh_values = mixed[:, wide + head :].astype(bf16)
+        fresh_keys = turn(mixed[:, query_width : query_width + head], key_gain_ref[...])
+        fresh_values = mixed[:, query_width + head :].astype(bf16)
         near_keys[member, :span, :] = fresh_keys
         near_values[member, :span, :] = fresh_values
-        present = lax.broadcasted_iota(jnp.int32, (span, head), 0) < valid_ref[member]
-        app_keys_ref[rows, :] = jnp.where(present, fresh_keys, jnp.zeros_like(fresh_keys))
-        app_values_ref[rows, :] = jnp.where(present, fresh_values, jnp.zeros_like(fresh_values))
-
+        fresh_keys_ref[rows, :] = fresh_keys
+        fresh_values_ref[rows, :] = fresh_values
+
+    by_head(1, head_values)
     enter(False)
     gather.finish()
     exchange_keys.relay()
@@ -622,46 +779,46 @@
     scatter.start_x(False)
     scatter.relay_x(True)
     scatter.relay_x(False)
+    scatter.cross()
     scatter.relay_z()
     scatter.finish_relays()
-    upper, lower = scatter.total()
-    for first, attn in ((0, upper), (32, lower)):
-        mid = tokens_ref[first : first + 32, :].astype(jnp.float32) + attn
-        middle[first : first + 32, :] = mid
-        mean_square = jnp.mean(mid * mid, axis=-1, keepdims=True)
-        rows_mid[row_window(me, first, 32), :] = (
-            mid * lax.rsqrt(mean_square + EPSILON) * mlp_gain_ref[...]
-        ).astype(jnp.bfloat16)
-    gather = Gather(mail, "g", rows_mid)
-    gather.start()
-    gather.relay_near()
+    wide = WideGather(mail, rows_mid)
+
+    def settle(half_index, attn):
+        first = half_index * HALF
+        mid = tokens_ref[first : first + HALF, :].astype(f32) + attn
+        middle[first : first + HALF, :] = mid
+        rows_mid[wide_window(0, 0, half_index), :] = rms(mid, mlp_gain_ref[...]).astype(bf16)
+        wide.start(half_index)
+
+    settle(0, scatter.upper())
+    settle(1, scatter.lower())
+    wide.relay()
     for load in loads[5:]:
         load.wait()
 
-    def feed(flip):
-        rows = half(flip)
-        both = jnp.dot(rows_mid[rows, :], w_both_vmem[...], preferred_element_type=jnp.float32)
+    def feed(first, count):
+        both = jnp.dot(
+            rows_mid[first : first + count, :], w_both_vmem[...], preferred_element_type=f32
+        )
         gate, up = both[:, :units], both[:, units:]
-        hidden = (gate / (1.0 + jnp.exp(-gate)) * up).astype(jnp.bfloat16)
-        part_two[rows, :] = jnp.dot(
-            hidden, w_down_vmem[...], preferred_element_type=jnp.float32
-        ).astype(jnp.bfloat16)
-
-    scatter = Scatter(mail, "b", part_two, *buffers_two)
-    gather.relay_far()
-    feed(False)
-    scatter.start_x(False)
-    gather.finish()
-    feed(True)
-    scatter.start_z()
-    scatter.start_x(True)
-    scatter.relay_x(False)
-    scatter.relay_x(True)
-    scatter.relay_z()
-    scatter.finish_relays()
-    upper, lower = scatter.total()
-    out_ref[0:32, :] = middle[0:32, :] + upper
-    out_ref[32:64, :] = middle[32:64, :] + lower
+        hidden = (gate / (1.0 + jnp.exp(-gate)) * up).astype(bf16)
+        part_two[first : first + count, :] = jnp.dot(
+            hidden, w_down_vmem[...], preferred_element_type=f32
+        ).astype(bf16)
+
+    back = WideScatter(mail, part_two, *buffers_two)
+    feed(0, OWN_ROWS)
+    wide.finish(0)
+    feed(OWN_ROWS, 4 * HALF)
+    back.start(0)
+    wide.finish(1)
+    feed(OWN_ROWS + 4 * HALF, 4 * HALF)
+    back.start(1)
+    back.relay()
+    for half_index in (0, 1):
+        first = half_index * HALF
+        out_ref[first : first + HALF, :] = middle[first : first + HALF, :] + back.total(half_index)
     mail.drain()
 
 
@@ -697,10 +854,15 @@
     smem = pl.BlockSpec(memory_space=pltpu.SMEM)
     vmem = pl.BlockSpec(memory_space=pltpu.VMEM)
     hbm = pl.BlockSpec(memory_space=pl.ANY)
-    arrived = (pages_keys.shape[0] * pages_keys.shape[1], PAGE, head)
-    relays = (2, 2, pages_keys.shape[1] // 2, PAGE, head)
+    own_pages, _, heads, _ = pages_keys.shape
+    arrived = (heads * own_pages, PAGE, head)
+    by_head = (heads, own_pages, PAGE, head)
+    relays = (2, 2, own_pages // 2, PAGE, head)
     buffers = [pltpu.VMEM(shape, bf16) for shape in SCATTER_BUFFERS]
-    copies = 2 * (SCATTER_COPIES + GATHER_COPIES + EXCHANGE_COPIES)
+    wide_buffers = [pltpu.VMEM(shape, bf16) for shape in WIDE_BUFFERS]
+    copies = (
+        SCATTER_COPIES + GATHER_COPIES + 2 * EXCHANGE_COPIES + WIDE_GATHER_COPIES + WIDE_SCATTER_COPIES
+    )
     cosine, sine = rope_offsets()
     return pl.pallas_call(
         layer_kernel,
@@ -721,9 +883,12 @@
             pltpu.VMEM((requests, query_rows, head), bf16),
             pltpu.VMEM((requests, NEAR, head), bf16),
             pltpu.VMEM((requests, NEAR, head), bf16),
-            pltpu.VMEM((rows_total, w_headgate.shape[1]), f32),
+            pltpu.VMEM((rows_total, w_headgate.shape[0]), f32),
             pltpu.VMEM(arrived, bf16),
             pltpu.VMEM(arrived, bf16),
+            pltpu.VMEM((2, *pages_keys.shape), bf16),
+            pltpu.VMEM(by_head, bf16),
+            pltpu.VMEM(by_head, bf16),
             pltpu.VMEM(relays, bf16),
             pltpu.VMEM(relays, bf16),
             pltpu.VMEM((WINDOW_TOKENS, head), bf16),
@@ -738,8 +903,8 @@
             pltpu.VMEM((rows_total, WIDTH), bf16),
             pltpu.VMEM(tokens.shape, f32),
             *buffers,
-            *buffers,
-            pltpu.SemaphoreType.DMA((10,)),
+            *wide_buffers,
+            pltpu.SemaphoreType.DMA((12,)),
             pltpu.SemaphoreType.DMA((copies,)),
             pltpu.SemaphoreType.DMA((copies,)),
         ],
@@ -758,7 +923,7 @@
         query_gain[None, :],
         key_gain[None, :],
         mlp_gain[None, :],
-        rope_bases(cached),
+        jnp.asarray(np.tile(rope_frequencies(), 2).astype(np.float32)[None, :]),
         jnp.asarray(cosine),
         jnp.asarray(sine),
         sink_keys,
@@ -800,12 +965,7 @@
     window,
     page_slot,
 ):
-    head_dim = query_gain.shape[0]
-
-    def by_head(pool):
-        return pool.transpose(2, 0, 1, 3)
-
-    output, app_keys, app_values = layer(
+    output, fresh_keys, fresh_values = layer(
         tokens,
         attn_gain,
         query_gain,
@@ -813,12 +973,12 @@
         mlp_gain,
         sink_key_cache[:, :, 0, :],
         sink_value_cache[:, :, 0, :],
-        by_head(pooled_keys),
-        by_head(pooled_values),
+        pooled_keys,
+        pooled_values,
         w_query,
         key_weight,
         value_weight,
-        jnp.pad(w_headgate, ((0, 0), (0, 128 - w_headgate.shape[1]))),
+        w_headgate.T,
         w_out,
         w_gate,
         w_up,
@@ -829,7 +989,13 @@
         window,
         page_slot[0],
     )
-    return (output, app_keys[:, None, :], app_values[:, None, :])
+    offsets = jnp.arange(SPAN_TOKENS, dtype=jnp.int32)
+    present = (offsets[None, :] < valid_length[:, None]).reshape(-1)[:, None, None]
+    app_keys, app_values = (
+        jnp.where(present, fresh[:, None, :], jnp.zeros((), fresh.dtype))
+        for fresh in (fresh_keys, fresh_values)
+    )
+    return (output, app_keys, app_values)
 
 
 def solution(mesh):

time: 136 us -> 127 us (0.934)
  local copies, waits for them, and re-layouts: 12.4 us -> 1.9 us
    transpose x1 -> x0, local copies, waits for them, and re-layouts: 4.9 us -> none  [by_head(): return pool.transpose(2, 0, 1, 3)]
    unnamed x4 -> x3, local copies, waits for them, and re-layouts: 6.01 us -> 1.88 us
    select_n x0 -> x1, other arithmetic: none -> 1.8 us  [body(): jnp.where(present, fresh[:, None, :], jnp.zeros((), fresh.dtype))]
where the time goes in v3:
time: 127 us
  Pallas kernels  122 us (96%)
  local copies, waits for them, and re-layouts  1.9 us (1%)
  other arithmetic  1.88 us (1%)
    pallas_call x1, Pallas kernels, layer(): pl.pallas_call(layer_kernel, out_shape=(jax.ShapeDtypeStruct(tokens.shape...  122 us

profile of v3, /device:TPU:16, one launch (start us, length us, event | category | flops | bytes accessed | tf_op | source)
XLA Modules:
  0.0 126.9 jit_solution(15824546466399081533)
XLA Ops:
  0.6 0.0 copy-start
  0.7 122.5 %layer.1 = (f32[64,2048]{1,0:T(8,128)}, bf16[512,128]{1,0:T(8,128)(2,1)}, bf16[512,128]{1,0:T(8,128)(2,1)}) custom-call(s32[2]{0:T(128)} %cached_ref.1, s32[2]{0:T(128)} %valid_ref.1, s32[2]{0:T(128)} %sinks_ref.1, s32[2]{0:T(128)} %reach_ref.1, s32[512]{0:T(512)} %bitcast.15, bf16[64,2048]{1,0:T(8,128)(2,1)} %tokens_ref.1, f32[1,2048]{1,0:T(1,128)} %bitcast.12, ...), custom_call_target="tpu_custom_call" | custom-call | tf_op jit(solution)/shard_map/layer/pallas_call | solution.py:867
  123.2 0.0 copy-done
  123.2 0.1 iota_compare_fusion
  123.3 1.8 %select_bitcast_fusion = (bf16[512,1,128]{2,0,1:T(8,128)(2,1)}, bf16[512,1,128]{2,0,1:T(8,128)(2,1)}) fusion(bf16[512,128]{1,0:T(8,128)(2,1)} %get-tuple-element.8, pred[512]{0:T(512)(128)(4,1)S(1)} %lt.23, bf16[512,128]{1,0:T(8,128)(2,1)} %get-tuple-element.7), kind=kLoop, calls=%fused_computation | loop fusion | flops 131072 | bytes 524800 | tf_op jit(solution)/shard_map/jit(_where)/select_n | solution.py:995
  125.1 1.9 %copy.29 = f32[64,2048]{1,0:T(8,128)} copy(f32[64,2048]{1,0:T(8,128)} %get-tuple-element.14) | data formatting | bytes 1048576
  (1 shorter events, 0.0 us)
Async XLA Ops:
  0.6 122.5 %copy-start = (s32[2]{0:T(128)S(1)}, s32[2]{0:T(128)}, u32[]{:S(2)}) copy-start(s32[2]{0:T(128)} %valid_ref.1) | copy-start | bytes 28

commit v4 on v3

--- a/solution.py
+++ b/solution.py
@@ -138,7 +138,7 @@
         add_into(self.part, ring_place(3, flip), 16, 16, self.h1.at[1, f])
         self.put(f"h2l{f}1", self.rows(3, flip, 16, 16), self.h2.at[1, f, 1], self.left)
 
-    def relay_z(self):
+    def relay_far(self):
         self.got("zb0", self.zb.at[0])
         add_into(self.part, ring_place(2, False), 32, 32, self.zb.at[0])
         self.put("b1r", self.rows(2, False, 32, 16), self.b1.at[0], self.right)
@@ -146,6 +146,8 @@
         self.got("zb1", self.zb.at[1])
         add_into(self.part, ring_place(1, False), 32, 32, self.zb.at[1])
         self.put("b2r1", self.rows(1, False, 48, 16), self.b2.at[0, 1], self.right)
+
+    def relay_z(self):
         self.got("zb2", self.zb.at[2])
         add_into(self.part, ring_place(3, False), 32, 32, self.zb.at[2])
         self.put("b2l0", self.rows(3, False, 32, 16), self.b2.at[1, 0], self.left)
@@ -577,8 +579,6 @@
         pltpu.make_async_copy(pages_keys_ref, raw_pages.at[0], load_sems.at[10]),
         pltpu.make_async_copy(pages_values_ref, raw_pages.at[1], load_sems.at[11]),
     ]
-    for load in raw_loads + loads:
-        load.start()
     meet_neighbours()
     mail = Mailer(send_sems, recv_sems)
     plane = lax.axis_index("tp") // 4
@@ -593,6 +593,8 @@
     ).astype(bf16)
     gather = Gather(mail, "n", rows_in)
     gather.start()
+    for load in raw_loads[:1] + loads[:4] + raw_loads[1:]:
+        load.start()
     for member in range(requests):
         near_keys[member, span:, :] = jnp.zeros((NEAR - span, head), bf16)
         near_values[member, span:, :] = jnp.zeros((NEAR - span, head), bf16)
@@ -661,17 +663,20 @@
     gather.finish()
     exchange_keys.relay()
     exchange_values.start()
+    for load in loads[4:]:
+        load.start()
     enter(True)
 
     def fetch(member, arrived):
+        count = 32
+
         def step(index, carry):
-            for part in range(8):
-                page = index * 8 + part
-                place = pl.ds(pl.multiple_of(page * PAGE, PAGE), PAGE)
-                window_rows[place, :] = arrived[slot_ref[member * pages + page]]
+            slots = [slot_ref[member * pages + index * count + part] for part in range(count)]
+            place = pl.ds(pl.multiple_of(index * count * PAGE, count * PAGE), count * PAGE)
+            window_rows[place, :] = jnp.concatenate([arrived[slot] for slot in slots], axis=0)
             return carry
 
-        lax.fori_loop(0, pages // 8, step, 0)
+        lax.fori_loop(0, pages // count, step, 0)
 
     def lane_tiles(values):
         return [values[:, k : k + 128] for k in range(0, values.shape[1], 128)]
@@ -779,6 +784,7 @@
     scatter.start_x(False)
     scatter.relay_x(True)
     scatter.relay_x(False)
+    scatter.relay_far()
     scatter.cross()
     scatter.relay_z()
     scatter.finish_relays()

time: 127 us -> 126 us (level)
  no operation moved by 1% of the time
where the time goes in v4:
time: 126 us
  Pallas kernels  122 us (97%)
  local copies, waits for them, and re-layouts  1.9 us (2%)
  other arithmetic  1.88 us (1%)
    pallas_call x1, Pallas kernels, layer(): pl.pallas_call(layer_kernel, out_shape=(jax.ShapeDtypeStruct(tokens.shape...  122 us

profile of v4, /device:TPU:16, one launch (start us, length us, event | category | flops | bytes accessed | tf_op | source)
XLA Modules:
  0.0 126.1 jit_solution(9020513405477301759)
XLA Ops:
  0.6 0.0 copy-start
  0.7 121.7 %layer.1 = (f32[64,2048]{1,0:T(8,128)}, bf16[512,128]{1,0:T(8,128)(2,1)}, bf16[512,128]{1,0:T(8,128)(2,1)}) custom-call(s32[2]{0:T(128)} %cached_ref.1, s32[2]{0:T(128)} %valid_ref.1, s32[2]{0:T(128)} %sinks_ref.1, s32[2]{0:T(128)} %reach_ref.1, s32[512]{0:T(512)} %bitcast.15, bf16[64,2048]{1,0:T(8,128)(2,1)} %tokens_ref.1, f32[1,2048]{1,0:T(1,128)} %bitcast.12, ...), custom_call_target="tpu_custom_call" | custom-call | tf_op jit(solution)/shard_map/layer/pallas_call | solution.py:873
  122.4 0.0 copy-done
  122.4 0.1 iota_compare_fusion
  122.5 1.8 %select_bitcast_fusion = (bf16[512,1,128]{2,0,1:T(8,128)(2,1)}, bf16[512,1,128]{2,0,1:T(8,128)(2,1)}) fusion(bf16[512,128]{1,0:T(8,128)(2,1)} %get-tuple-element.8, pred[512]{0:T(512)(128)(4,1)S(1)} %lt.23, bf16[512,128]{1,0:T(8,128)(2,1)} %get-tuple-element.7), kind=kLoop, calls=%fused_computation | loop fusion | flops 131072 | bytes 524800 | tf_op jit(solution)/shard_map/jit(_where)/select_n | solution.py:1001
  124.3 1.9 %copy.29 = f32[64,2048]{1,0:T(8,128)} copy(f32[64,2048]{1,0:T(8,128)} %get-tuple-element.14) | data formatting | bytes 1048576
  (1 shorter events, 0.0 us)
Async XLA Ops:
  0.6 121.7 %copy-start = (s32[2]{0:T(128)S(1)}, s32[2]{0:T(128)}, u32[]{:S(2)}) copy-start(s32[2]{0:T(128)} %valid_ref.1) | copy-start | bytes 28
